TPU v7x, 512 devices: a whole 4x4x16 slice. The times are simulated.
512 devices in a mesh: lead: 4 (over x_hi, core), lat: 32 (over x_lo, z), lon: 4 (over y).
Axes of the slice: x: 4 (x_hi: 2, x_lo: 2; x = x_hi * 2 + x_lo), y: 4, z: 16, core: 2. Of those that a mesh axis runs over, the one named last changes fastest.
Arguments:
- head_grads: bfloat16 [8, 8, 128, 128, 128], P('lead', None, 'lat', 'lon'), may hold values from -6 to 6
- head_weights: bfloat16 [8, 9, 256, 128], P('lead'), may hold values from -0.0625 to 0.0625
- encoder_input: bfloat16 [8, 128, 128, 128], P('lead', 'lat', 'lon'), may hold values from -6 to 6
- pre_first: bfloat16 [8, 128, 128, 256], P('lead', 'lat', 'lon'), may hold values from -8 to 8
- pre_second: bfloat16 [8, 128, 128, 256], P('lead', 'lat', 'lon'), may hold values from -8 to 8
- w_first: bfloat16 [9, 128, 256], replicated, may hold values from -0.1875 to 0.1875
- w_second: bfloat16 [9, 256, 256], replicated, may hold values from -0.125 to 0.125
Outputs:
- input_grad: bfloat16 [8, 128, 128, 128], P('lead', 'lat', 'lon')
- weight_grad_first: float32 [294912], P(('lat', 'lon'))
- weight_grad_second: float32 [589824], P(('lat', 'lon'))
All inputs are finite; a program needn't handle non-finite values.
Results may differ from a plain program's by a relative error of at most 0.022.
Values may be sent and summed in bfloat16 or wider, within the bound.
A program may use at most 64 MiB of HBM per device.

v0:
```python
import math

import jax
import jax.numpy as jnp
from jax import lax
from jax.sharding import PartitionSpec as P

OFFSETS = [(-1, -1), (-1, 0), (-1, 1), (0, -1), (0, 0), (0, 1), (1, -1), (1, 0), (1, 1)]


def with_halo(block, sides, width, periodic):
    for axis, dim in sides:
        count = lax.axis_size(axis)
        forward = [(i, i + 1) for i in range(count - 1)]
        if periodic:
            forward.append((count - 1, 0))
        backward = [(target, source) for source, target in forward]
        low = lax.ppermute(
            lax.slice_in_dim(block, block.shape[dim] - width, None, axis=dim), axis, forward
        )
        high = lax.ppermute(lax.slice_in_dim(block, 0, width, axis=dim), axis, backward)
        block = jnp.concatenate([low, block, high], axis=dim)
    return block


def gelu_value(values):
    return 0.5 * values * (1.0 + lax.erf(values * 0.7071067811865476))


def gelu_slope(values):
    return (
        0.5 * (1.0 + lax.erf(values * 0.7071067811865476))
        + values * jnp.exp(-0.5 * values * values) * 0.3989422804014327
    )


def widen(source):
    extended = with_halo(source, (("lon", 2),), 1, True)
    return with_halo(extended, (("lat", 1),), 1, False)


def window(padded, step_row, step_col):
    height = padded.shape[-3] - 2
    breadth = padded.shape[-2] - 2
    return padded[
        ..., 1 + step_row : 1 + step_row + height, 1 + step_col : 1 + step_col + breadth, :
    ]


def per_device(head_grads, head_weights, encoder_input, pre_first, pre_second, w_first, w_second):
    heads_here, batch_all, height, breadth, head_channels = head_grads.shape
    samples = encoder_input.shape[0]
    latent_width = head_weights.shape[2]
    merged = head_grads.reshape(heads_here * batch_all, height, breadth, head_channels)
    padded_heads = widen(merged).reshape(
        heads_here, batch_all, height + 2, breadth + 2, head_channels
    )
    summed = jnp.zeros(
        (samples * lax.axis_size("lead"), height, breadth, latent_width), jnp.float32
    )
    for latent_offset, (latent_step_row, latent_step_col) in enumerate(OFFSETS):
        moved = window(padded_heads, -latent_step_row, -latent_step_col)
        summed = summed + jnp.einsum(
            "hbrcj,hdj->brcd",
            moved,
            head_weights[:, latent_offset],
            preferred_element_type=jnp.float32,
        )
    latent_grad = lax.psum_scatter(
        summed.astype(jnp.bfloat16), "lead", scatter_dimension=0, tiled=True
    ).astype(jnp.float32)
    pre_two = pre_second.astype(jnp.float32)
    pre_one = pre_first.astype(jnp.float32)
    da_second = (latent_grad * gelu_slope(pre_two)).astype(jnp.bfloat16)
    act_first = gelu_value(pre_one).astype(jnp.bfloat16)
    padded_act = widen(act_first)
    padded_input = widen(encoder_input)
    padded_second = widen(da_second)
    grad_second = []
    linear_first = jnp.zeros((samples, height, breadth, latent_width), jnp.float32)
    for offset, (step_row, step_col) in enumerate(OFFSETS):
        grad_second.append(
            jnp.einsum(
                "brci,brcd->id",
                window(padded_act, step_row, step_col),
                da_second,
                preferred_element_type=jnp.float32,
            )
        )
        linear_first = linear_first + jnp.einsum(
            "brcd,id->brci",
            window(padded_second, -step_row, -step_col),
            w_second[offset],
            preferred_element_type=jnp.float32,
        )
    da_first = (linear_first * gelu_slope(pre_one)).astype(jnp.bfloat16)
    padded_first = widen(da_first)
    grad_first = []
    input_sum = jnp.zeros((samples, height, breadth, w_first.shape[1]), jnp.float32)
    for offset, (step_row, step_col) in enumerate(OFFSETS):
        grad_first.append(
            jnp.einsum(
                "brcj,brcd->jd",
                window(padded_input, step_row, step_col),
                da_first,
                preferred_element_type=jnp.float32,
            )
        )
        input_sum = input_sum + jnp.einsum(
            "brcd,jd->brcj",
            window(padded_first, -step_row, -step_col),
            w_first[offset],
            preferred_element_type=jnp.float32,
        )
    input_grad = input_sum.astype(jnp.bfloat16)
    cells_total = (
        samples
        * lax.axis_size("lead")
        * height
        * lax.axis_size("lat")
        * breadth
        * lax.axis_size("lon")
    )
    norm_factor = 1.0 / math.sqrt(cells_total)
    flat_first = (jnp.stack(grad_first) * norm_factor).reshape(-1)
    flat_second = (jnp.stack(grad_second) * norm_factor).reshape(-1)
    whole_first, whole_second = (
        lax.psum(flat_first.astype(jnp.bfloat16), "lead").astype(jnp.float32),
        lax.psum(flat_second.astype(jnp.bfloat16), "lead").astype(jnp.float32),
    )
    result_first, result_second = (
        lax.psum_scatter(whole_first, ("lat", "lon"), scatter_dimension=0, tiled=True),
        lax.psum_scatter(whole_second, ("lat", "lon"), scatter_dimension=0, tiled=True),
    )
    return (input_grad, result_first, result_second)


def solution(mesh):
    in_specs = (
        P("lead", None, "lat", "lon", None),
        P("lead", None, None, None),
        P("lead", "lat", "lon", None),
        P("lead", "lat", "lon", None),
        P("lead", "lat", "lon", None),
        P(),
        P(),
    )
    out_specs = (P("lead", "lat", "lon", None), P(("lat", "lon")), P(("lat", "lon")))
    return jax.shard_map(
        per_device, mesh=mesh, in_specs=in_specs, out_specs=out_specs, check_vma=False
    )
```

profile of v0, /device:TPU:2, one launch (start us, length us, event | category | flops | bytes accessed | tf_op | source)
XLA Modules:
  0.0 843.0 jit_solution(9377522992387471817)
XLA Ops:
  7.2 1.4 copy.154
  8.6 3.5 collective-permute-start
  12.1 3.6 collective-permute-start.1
  15.7 2.0 collective-permute-done.1
  17.8 3.8 collective-permute-start.2
  21.6 9.5 %collective-permute-start.3 = (bf16[16,1,34,128]{3,0,2,1:T(8,128)(2,1)S(1)}, bf16[16,1,34,128]{3,0,2,1:T(8,128)(2,1)S(1)}, u32[]{:S(2)}, u32[]{:S(2)}) collective-permute-start(bf16[16,1,34,128]{3,0,2,1:T(8,128)(2,1)S(1)} %get-tuple-element.17), channel_id=1, source_target_pairs={{4,0},{8,4},{12,8},{16,12},{20,16},{24,20},{28,24},{32,28},{36,32}... | collective-permute-start | bytes 417800 | tf_op jit(solution)/shard_map/ppermute | solution.py:21
  31.1 1.1 collective-permute-done.2
  32.2 1.5 collective-permute-done.3
  33.8 0.7 fusion.175
  34.5 0.5 copy-done.2
  35.1 0.3 convolution_bitcast_fusion
  35.4 0.3 convolution_bitcast_fusion.1
  35.8 0.3 convolution_bitcast_fusion.2
  36.1 0.3 convolution_bitcast_fusion.3
  36.5 0.3 convolution_bitcast_fusion.4
  37.6 0.3 convolution_bitcast_fusion.7
  37.9 1.5 fusion.8
  39.5 3.5 collective-permute-start.12
  43.0 3.6 collective-permute-start.13
  46.7 2.3 collective-permute-start.16
  49.0 4.8 collective-permute-start.17
  53.7 1.3 dynamic-slice
  56.4 1.9 collective-permute-start.14
  58.3 6.5 collective-permute-start.15
  64.8 1.9 collective-permute-start.18
  66.8 6.0 collective-permute-start.19
  72.9 1.6 collective-permute-done.19
  74.5 7.0 reduce-scatter.2.cloned.1.call-done
  81.6 1.0 fusion.65
  85.1 4.8 collective-permute-start.5
  89.9 1.9 collective-permute-start.4
  92.0 2.2 copy.134
  94.3 2.4 collective-permute-done.4
  96.7 6.8 collective-permute-start.6
  103.5 1.9 collective-permute-start.7
  105.7 5.8 collective-permute-done.7
  115.3 2.8 collective-permute-start.9
  118.1 3.1 collective-permute-start.8
  121.3 1.4 copy.133
  122.7 2.1 collective-permute-done.8
  124.9 1.9 collective-permute-start.10
  126.8 3.9 collective-permute-start.11
  130.9 4.0 collective-permute-done.11
  136.1 0.8 fusion.41
  137.0 48.8 %all-reduce.7.cloned.1.call-done = (bf16[294912]{0:T(1024)(128)(2,1)}, bf16[589824]{0:T(1024)(128)(2,1)}) async-done(((bf16[294912]{0:T(1024)(128)(2,1)}, bf16[589824]{0:T(1024)(128)(2,1)}), (bf16[294912]{0:T(1024)(128)(2,1)}, bf16[589824]{0:T(1024)(128)(2,1)})) %all-reduce.7.cloned.1.call-update) | async-done | bytes 1769488 | tf_op jit(solution)/shard_map/psum | solution.py:128
  185.7 649.0 %all-reduce.8 = (f32[294912]{0:T(1024)S(1)}, f32[589824]{0:T(1024)S(1)}) all-reduce(bf16[294912]{0:T(1024)(128)(2,1)} %get-tuple-element.5, bf16[589824]{0:T(1024)(128)(2,1)} %get-tuple-element.6), channel_id=3, replica_groups=mesh['lead'=4,'lat'=32,'lon'=4] {'lat','lon'}, use_global_device_ids=true, to_apply=%region_2.0.clone | all-reduce | flops 884736 | bytes 5308416
  834.8 0.7 dynamic-slice.3
  835.5 0.7 dynamic-slice.1
  (82 shorter events, 9.4 us)
Async XLA Ops:
  7.2 74.4 %reduce-scatter.2.cloned.1.call-start = ((), (), s32[]{:S(2)}) async-start(), calls=%async_computation.1 | async-start | bytes 655360 | tf_op jit(solution)/shard_map/reduce_scatter | solution.py:69
  8.6 7.1 collective-permute-start
  12.1 5.6 collective-permute-start.1
  17.8 14.4 %collective-permute-start.2 = (bf16[16,1,34,128]{3,0,2,1:T(8,128)(2,1)S(1)}, bf16[16,1,34,128]{3,0,2,1:T(8,128)(2,1)S(1)}, u32[]{:S(2)}, u32[]{:S(2)}) collective-permute-start(bf16[16,1,34,128]{3,0,2,1:T(8,128)(2,1)S(1)} %get-tuple-element.16), channel_id=1, source_target_pairs={{0,4},{4,8},{8,12},{12,16},{16,20},{20,24},{24,28},{28,32},{32,36}... | collective-permute-start | bytes 417800 | tf_op jit(solution)/shard_map/ppermute | solution.py:18
  21.6 12.1 %collective-permute-start.3 = (bf16[16,1,34,128]{3,0,2,1:T(8,128)(2,1)S(1)}, bf16[16,1,34,128]{3,0,2,1:T(8,128)(2,1)S(1)}, u32[]{:S(2)}, u32[]{:S(2)}) collective-permute-start(bf16[16,1,34,128]{3,0,2,1:T(8,128)(2,1)S(1)} %get-tuple-element.17), channel_id=1, source_target_pairs={{4,0},{8,4},{12,8},{16,12},{20,16},{24,20},{28,24},{32,28},{36,32}... | collective-permute-start | bytes 417800 | tf_op jit(solution)/shard_map/ppermute | solution.py:21
  33.8 1.3 copy-start.2
  37.9 1.6 copy-start
  37.9 8.6 %copy-start.3 = (bf16[2,4,32,256]{3,2,1,0:T(8,128)(2,1)S(1)}, bf16[2,4,32,256]{3,2,1,0:T(8,128)(2,1)}, u32[]{:S(2)}) copy-start(bf16[2,4,32,256]{3,2,1,0:T(8,128)(2,1)} %param.10) | copy-start | bytes 393220
  39.4 42.2 %copy-start.5 = (bf16[2,4,32,256]{3,2,1,0:T(8,128)(2,1)S(1)}, bf16[2,4,32,256]{3,2,1,0:T(8,128)(2,1)}, u32[]{:S(2)}) copy-start(bf16[2,4,32,256]{3,2,1,0:T(8,128)(2,1)} %param.11) | copy-start | bytes 393220
  39.4 146.3 %all-reduce.7.cloned.1.call-start = ((), (), s32[]{:S(2)}) async-start(), calls=%async_computation.2 | async-start | bytes 3538944 | tf_op jit(solution)/shard_map/psum | solution.py:128
  39.5 16.8 %collective-permute-start.12 = (bf16[2,4,1,128]{3,2,1,0:T(2,128)(2,1)S(1)}, bf16[2,4,1,128]{3,2,1,0:T(2,128)(2,1)S(1)}, u32[]{:S(2)}, u32[]{:S(2)}) collective-permute-start(bf16[2,4,1,128]{3,2,1,0:T(2,128)(2,1)S(1)} %get-tuple-element.42), channel_id=1, source_target_pairs={{0,1},{1,2},{2,3},{3,0},{4,5},{5,6},{6,7},{7,4},{8,9},{9,10},{10,1... | collective-permute-start | bytes 6152 | tf_op jit(solution)/shard_map/ppermute | solution.py:18
  43.0 13.3 %collective-permute-start.13 = (bf16[2,4,1,128]{3,2,1,0:T(2,128)(2,1)S(1)}, bf16[2,4,1,128]{3,2,1,0:T(2,128)(2,1)S(1)}, u32[]{:S(2)}, u32[]{:S(2)}) collective-permute-start(bf16[2,4,1,128]{3,2,1,0:T(2,128)(2,1)S(1)} %get-tuple-element.43), channel_id=1, source_target_pairs={{1,0},{2,1},{3,2},{0,3},{5,4},{6,5},{7,6},{4,7},{9,8},{10,9},{11,1... | collective-permute-start | bytes 6152 | tf_op jit(solution)/shard_map/ppermute | solution.py:21
  46.7 18.1 %collective-permute-start.16 = (bf16[2,4,1,256]{3,2,1,0:T(2,128)(2,1)S(1)}, bf16[2,4,1,256]{3,2,1,0:T(2,128)(2,1)S(1)}, u32[]{:S(2)}, u32[]{:S(2)}) collective-permute-start(bf16[2,4,1,256]{3,2,1,0:T(2,128)(2,1)S(1)} %get-tuple-element.32), channel_id=1, source_target_pairs={{0,1},{1,2},{2,3},{3,0},{4,5},{5,6},{6,7},{7,4},{8,9},{9,10},{10,1... | collective-permute-start | bytes 12296 | tf_op jit(solution)/shard_map/ppermute | solution.py:18
  49.0 15.8 %collective-permute-start.17 = (bf16[2,4,1,256]{3,2,1,0:T(2,128)(2,1)S(1)}, bf16[2,4,1,256]{3,2,1,0:T(2,128)(2,1)S(1)}, u32[]{:S(2)}, u32[]{:S(2)}) collective-permute-start(bf16[2,4,1,256]{3,2,1,0:T(2,128)(2,1)S(1)} %get-tuple-element.33), channel_id=1, source_target_pairs={{1,0},{2,1},{3,2},{0,3},{5,4},{6,5},{7,6},{4,7},{9,8},{10,9},{11,1... | collective-permute-start | bytes 12296 | tf_op jit(solution)/shard_map/ppermute | solution.py:21
  56.4 16.4 %collective-permute-start.14 = (bf16[2,1,34,128]{3,2,1,0:T(8,128)(2,1)S(1)}, bf16[2,1,34,128]{3,2,1,0:T(8,128)(2,1)S(1)}, u32[]{:S(2)}, u32[]{:S(2)}) collective-permute-start(bf16[2,1,34,128]{3,2,1,0:T(8,128)(2,1)S(1)} %get-tuple-element.41), channel_id=1, source_target_pairs={{0,4},{4,8},{8,12},{12,16},{16,20},{20,24},{24,28},{28,32},{32,36}... | collective-permute-start | bytes 52232 | tf_op jit(solution)/shard_map/ppermute | solution.py:18
  58.3 14.5 %collective-permute-start.15 = (bf16[2,1,34,128]{3,2,1,0:T(8,128)(2,1)S(1)}, bf16[2,1,34,128]{3,2,1,0:T(8,128)(2,1)S(1)}, u32[]{:S(2)}, u32[]{:S(2)}) collective-permute-start(bf16[2,1,34,128]{3,2,1,0:T(8,128)(2,1)S(1)} %get-tuple-element.40), channel_id=1, source_target_pairs={{4,0},{8,4},{12,8},{16,12},{20,16},{24,20},{28,24},{32,28},{36,32}... | collective-permute-start | bytes 52232 | tf_op jit(solution)/shard_map/ppermute | solution.py:21
  64.8 8.1 collective-permute-start.18
  66.8 7.7 collective-permute-start.19
  84.8 7.0 copy-start.1
  85.1 9.2 %collective-permute-start.5 = (bf16[2,4,1,256]{3,2,1,0:T(2,128)(2,1)S(1)}, bf16[2,4,1,256]{3,2,1,0:T(2,128)(2,1)S(1)}, u32[]{:S(2)}, u32[]{:S(2)}) collective-permute-start(bf16[2,4,1,256]{3,2,1,0:T(2,128)(2,1)S(1)} %get-tuple-element.37), channel_id=1, source_target_pairs={{1,0},{2,1},{3,2},{0,3},{5,4},{6,5},{7,6},{4,7},{9,8},{10,9},{11,1... | collective-permute-start | bytes 12296 | tf_op jit(solution)/shard_map/ppermute | solution.py:21
  89.9 6.8 collective-permute-start.4
  96.7 9.0 %collective-permute-start.6 = (bf16[2,1,34,256]{3,2,1,0:T(8,128)(2,1)S(1)}, bf16[2,1,34,256]{3,2,1,0:T(8,128)(2,1)S(1)}, u32[]{:S(2)}, u32[]{:S(2)}) collective-permute-start(bf16[2,1,34,256]{3,2,1,0:T(8,128)(2,1)S(1)} %get-tuple-element.30), channel_id=1, source_target_pairs={{4,0},{8,4},{12,8},{16,12},{20,16},{24,20},{28,24},{32,28},{36,32}... | collective-permute-start | bytes 104456 | tf_op jit(solution)/shard_map/ppermute | solution.py:21
  103.5 8.0 collective-permute-start.7
  114.7 6.4 copy-start.4
  115.3 7.4 collective-permute-start.9
  118.1 6.8 collective-permute-start.8
  124.9 6.0 collective-permute-start.10
  126.8 8.1 collective-permute-start.11
Sparse Core Ops, SparseCore 0:
  39.5 41.9 reduce-scatter.1
  122.8 62.8 all-reduce.6
where the time goes:
time: 844 us; the launch traced here: 843 us
  blocking collectives  649 us (77%)
  starting transfers between devices  78 us (9%)
  waiting for transfers between devices  76.3 us (9%)
  between operations  16.1 us (2%)
  matrix products  12.5 us (1%)
  local copies, waits for them, and re-layouts  8.96 us (1%)
    unnamed x1, blocking collectives  649 us
    ppermute x10, starting transfers between devices, with_halo(): lax.ppermute(lax.slice_in_dim(block, 0, width, axis=dim), axis, backward)  50.2 us
    psum x1, waiting for transfers between devices, per_device(): lax.psum(flat_first.astype(jnp.bfloat16), 'lead').astype(jnp.float32)  48.8 us
    ppermute x10, starting transfers between devices, with_halo(): lax.ppermute(lax.slice_in_dim(block, block.shape[dim] - width, None, axis...  27.7 us
  transfers between devices with their start and end apart: 22, of which 10 were waited for; matrix products, arithmetic and copies ran while one was open for 1% of the time, Pallas kernels for 0%

commit v1 on v0

v1 whole, which is shorter than its diff:
```python
import functools
import math

import jax
import jax.numpy as jnp
from jax import lax
from jax.experimental import pallas as pl
from jax.experimental.pallas import tpu as pltpu
from jax.sharding import PartitionSpec as P

OFFSETS = [(-1, -1), (-1, 0), (-1, 1), (0, -1), (0, 0), (0, 1), (1, -1), (1, 0), (1, 1)]
MESH = pl.DeviceIdType.MESH
BF = jnp.bfloat16
F32 = jnp.float32
NT = (((1,), (1,)), ((), ()))
NN = (((1,), (0,)), ((), ()))
UNIT = 8


def gelu_value(values):
    return 0.5 * values * (1.0 + lax.erf(values * 0.7071067811865476))


def gelu_slope(values):
    return (
        0.5 * (1.0 + lax.erf(values * 0.7071067811865476))
        + values * jnp.exp(-0.5 * values * values) * 0.3989422804014327
    )


def matmul(a, b, dims):
    return lax.dot_general(a, b, dims, preferred_element_type=F32)


class Place:
    def __init__(self):
        self.lead = lax.axis_index("lead")
        self.lat = lax.axis_index("lat")
        self.lon = lax.axis_index("lon")
        self.n_lead = lax.axis_size("lead")
        self.n_lat = lax.axis_size("lat")
        self.n_lon = lax.axis_size("lon")
        self.planes = self.n_lead * self.n_lon
        self.fold = self.n_lat // self.planes
        self.x = self.lat // self.planes
        self.z = self.lat % self.planes
        self.seat = self.x * self.planes + self.lon * self.n_lead + self.lead
        self.has_low = self.lat > 0
        self.has_high = self.lat < self.n_lat - 1

    def seat_device(self, seat):
        rest = seat % self.planes
        lat = (seat // self.planes) * self.planes + self.z
        return (rest % self.n_lead, lat, rest // self.n_lead)

    def near(self, rows, cols):
        return (self.lead, self.lat + rows, (self.lon + cols + self.n_lon) % self.n_lon)


class Halo:
    def __init__(self, here, rows_out, rows_in, field, edge, ring, send, recv):
        self.here, self.field, self.edge, self.ring = here, field, edge, ring
        self.units = edge.shape[1]
        self.rows = field.shape[0] - 2
        self.batch = field.shape[1]
        self.cols = field.shape[2]
        copies = []
        slot = 0
        for high in (0, 1):
            step = 1 if high == 0 else -1
            sends = here.has_high if high == 0 else here.has_low
            takes = here.has_low if high == 0 else here.has_high
            for source, target in zip(rows_out[high], rows_in[high]):
                copies.append((sends, takes, source, target, here.near(step, 0), slot))
                slot += 1
        self.row_count = slot
        body = pl.ds(1, self.units)
        for right in (0, 1):
            step = 1 if right == 0 else -1
            source = edge.at[1 - right]
            copies.append((None, None, source, ring.at[right, body], here.near(0, step), slot))
            slot += 1
        for high in (0, 1):
            for right in (0, 1):
                row_step = 1 if high == 0 else -1
                col_step = 1 if right == 0 else -1
                sends = here.has_high if high == 0 else here.has_low
                takes = here.has_low if high == 0 else here.has_high
                source = edge.at[1 - right, self.units - 1 if high == 0 else 0]
                target = ring.at[right, 0 if high == 0 else self.units + 1]
                copies.append((sends, takes, source, target, here.near(row_step, col_step), slot))
                slot += 1
        self.copies = [
            (
                sends,
                takes,
                pltpu.make_async_remote_copy(
                    src_ref=source,
                    dst_ref=target,
                    send_sem=send.at[number],
                    recv_sem=recv.at[number],
                    device_id=device,
                    device_id_type=MESH,
                ),
            )
            for sends, takes, source, target, device, number in copies
        ]

    def run(self, items, which, name):
        for item in items:
            if item[which] is None:
                getattr(item[2], name)()
            else:
                pl.when(item[which])(getattr(item[2], name))

    def start_rows(self):
        self.run(self.copies[: self.row_count], 0, "start")

    def start_columns(self):
        self.run(self.copies[self.row_count :], 0, "start")

    def wait_recv(self):
        self.run(self.copies, 1, "wait_recv")

    def wait_send(self):
        self.run(self.copies, 0, "wait_send")

    def clear(self):
        def low():
            self.field[0] = jnp.zeros(self.field.shape[1:], self.field.dtype)
            for side in (0, 1):
                self.ring[side, 0] = jnp.zeros(self.ring.shape[2:], F32)

        def high():
            self.field[self.rows + 1] = jnp.zeros(self.field.shape[1:], self.field.dtype)
            for side in (0, 1):
                self.ring[side, self.units + 1] = jnp.zeros(self.ring.shape[2:], F32)

        pl.when(jnp.logical_not(self.here.has_low))(low)
        pl.when(jnp.logical_not(self.here.has_high))(high)

    def place(self, row, b):
        flat = row * self.batch + b
        return flat // UNIT, flat % UNIT

    def take_edges(self):
        for row in range(self.rows):
            for b in range(self.batch):
                unit, sub = self.place(row, b)
                block = self.field[1 + row, b].astype(F32)
                self.edge[0, unit, sub : sub + 1] = block[0:1]
                self.edge[1, unit, sub : sub + 1] = block[self.cols - 1 : self.cols]

    def ring_row(self, side, ext, b):
        if ext == 0:
            unit, sub = self.place(self.rows - 1, b)
            unit = 0
        elif ext == self.rows + 1:
            unit, sub = self.place(0, b)
            unit = self.units + 1
        else:
            unit, sub = self.place(ext - 1, b)
            unit = unit + 1
        return self.ring[side, unit, sub : sub + 1]

    def spread(self, base, out):
        for ext in range(self.rows + 2):
            for b in range(self.batch):
                block = base[ext, b].astype(F32)
                column = lax.broadcasted_iota(jnp.int32, block.shape, 0)
                behind = jnp.where(
                    column == 0, self.ring_row(0, ext, b), pltpu.roll(block, 1, 0)
                )
                ahead = jnp.where(
                    column == self.cols - 1,
                    self.ring_row(1, ext, b),
                    pltpu.roll(block, self.cols - 1, 0),
                )
                out[0, ext, b] = behind.astype(BF)
                out[1, ext, b] = ahead.astype(BF)


def window(base, spread, step_row, step_col, rows, batch=None):
    row = pl.ds(1 + step_row, rows)
    if step_col == 0:
        view = base[row] if batch is None else base[row, batch]
    else:
        side = 0 if step_col < 0 else 1
        view = spread[side, row] if batch is None else spread[side, row, batch]
    return view.reshape(-1, view.shape[-1])


def kernel(
    norm,
    heads_hbm, head_w_hbm, input_hbm, first_hbm, second_hbm, w_first_hbm, w_second_hbm,
    grad_out, first_out, second_out,
    xh, xh2, eh, rh, head_w,
    xp, xa, xa2, ep, rp,
    xe, xe2, ee, re,
    x2, x22, e2, r2,
    x1, x12, e1, r1,
    pre_two, slope_two, slope_one, w_one, w_two,
    part, parts_in,
    act_t, input_t,
    s1b, q1b, s2b, q2b, s1a, q1a, s2a, q2a,
    grad_stage,
    load_sem, halo_send, halo_recv, lead_send, lead_recv,
    p1_send, p1_recv, p2_send, p2_recv,
):
    here = Place()
    n_lead, planes, n_lon = here.n_lead, here.planes, here.n_lon
    seats = here.fold * planes
    heads, batch_all, rows, cols, head_width = heads_hbm.shape
    samples = input_hbm.shape[0]
    cells = samples * rows * cols

    loads = {}
    count = 0

    def load(key, source, target):
        nonlocal count
        copy = pltpu.make_async_copy(source, target, load_sem.at[count])
        copy.start()
        loads.setdefault(key, []).append(copy)
        count += 1

    for row in range(rows):
        for h in range(heads):
            lanes = pl.ds(h * head_width, head_width)
            load("heads", heads_hbm.at[h, :, row], xh.at[1 + row, :, :, lanes])
    for row in range(rows):
        load("first", first_hbm.at[:, row], xp.at[1 + row])
        load("input", input_hbm.at[:, row], xe.at[1 + row])
    for h in range(heads):
        load("head_w", head_w_hbm.at[h], head_w.at[:, :, pl.ds(h * head_width, head_width)])
    for row in range(rows):
        load("second", second_hbm.at[:, row], pre_two.at[row])
    load("w_two", w_second_hbm, w_two)
    load("w_one", w_first_hbm, w_one)

    def ready(key):
        for copy in loads[key]:
            copy.wait()

    lane = [pl.ds(h * head_width, head_width) for h in range(heads)]
    halo_h = Halo(
        here,
        [[heads_hbm.at[h, :, rows - 1] for h in range(heads)], [heads_hbm.at[h, :, 0] for h in range(heads)]],
        [[xh.at[0, :, :, lane[h]] for h in range(heads)], [xh.at[rows + 1, :, :, lane[h]] for h in range(heads)]],
        xh, eh, rh, halo_send.at[0], halo_recv.at[0],
    )
    halo_p = Halo(
        here,
        [[first_hbm.at[:, rows - 1]], [first_hbm.at[:, 0]]],
        [[xp.at[0]], [xp.at[rows + 1]]],
        xp, ep, rp, halo_send.at[1], halo_recv.at[1],
    )
    halo_e = Halo(
        here,
        [[input_hbm.at[:, rows - 1]], [input_hbm.at[:, 0]]],
        [[xe.at[0]], [xe.at[rows + 1]]],
        xe, ee, re, halo_send.at[2], halo_recv.at[2],
    )
    halo_2 = Halo(
        here, [[x2.at[rows]], [x2.at[1]]], [[x2.at[0]], [x2.at[rows + 1]]],
        x2, e2, r2, halo_send.at[3], halo_recv.at[3],
    )
    halo_1 = Halo(
        here, [[x1.at[rows]], [x1.at[1]]], [[x1.at[0]], [x1.at[rows + 1]]],
        x1, e1, r1, halo_send.at[4], halo_recv.at[4],
    )

    barrier = pltpu.get_barrier_semaphore()

    def greet(device):
        pl.semaphore_signal(barrier, inc=1, device_id=device, device_id_type=MESH)

    for has, step in ((here.has_low, -1), (here.has_high, 1)):

        def greet_rows(step=step):
            for col in (-1, 0, 1):
                greet(here.near(step, col))

        pl.when(has)(greet_rows)

    @pl.loop(1, seats)
    def _(j):
        greet(here.seat_device((here.seat + j) % seats))

    feeder_lon = here.z // n_lead
    feeder_lead = here.z % n_lead
    target_z = here.lon * n_lead + here.lead
    own_feed = jnp.logical_and(here.lon == feeder_lon, here.lead == feeder_lead)

    @pl.loop(0, planes)
    def _(z):
        @pl.when(jnp.logical_not(jnp.logical_and(own_feed, z == here.z)))
        def _():
            greet((feeder_lead, here.x * planes + z, feeder_lon))

    greetings = (
        seats - 1
        + jnp.where(here.has_low, 3, 0)
        + jnp.where(here.has_high, 3, 0)
        + planes
        - jnp.where(here.z == target_z, 1, 0)
    )

    halo_h.clear()
    halo_p.clear()
    halo_e.clear()
    halo_2.clear()
    halo_1.clear()
    ready("heads")
    halo_h.take_edges()
    pl.semaphore_wait(barrier, greetings)
    halo_h.start_rows()
    halo_h.start_columns()
    ready("first")
    halo_p.take_edges()
    halo_p.start_rows()
    halo_p.start_columns()
    ready("input")
    halo_e.take_edges()
    halo_e.start_rows()
    halo_e.start_columns()
    ready("head_w")

    halo_h.wait_recv()
    halo_h.spread(xh, xh2)

    def lead_copy(owner):
        return pltpu.make_async_remote_copy(
            src_ref=part.at[owner],
            dst_ref=parts_in.at[here.lead],
            send_sem=lead_send.at[owner],
            recv_sem=lead_recv.at[here.lead],
            device_id=(owner, here.lat, here.lon),
            device_id_type=MESH,
        )

    @pl.loop(0, n_lead)
    def _(j):
        owner = (here.lead + n_lead - 1 - j) % n_lead
        batch = pl.ds(owner * samples, samples)
        total = jnp.zeros((cells, head_w.shape[1]), F32)
        for k, (u, v) in enumerate(OFFSETS):
            total += matmul(window(xh, xh2, -u, -v, rows, batch), head_w[k], NT)
        part[owner] = total.astype(BF).reshape(part.shape[1:])

        @pl.when(owner != here.lead)
        def _():
            lead_copy(owner).start()

    ready("second")
    for row in range(rows):
        slope_two[row] = gelu_slope(pre_two[row].astype(F32))
        slope_one[row] = gelu_slope(xp[1 + row].astype(F32))
    halo_p.wait_recv()
    for row in range(rows + 2):
        xa[row] = gelu_value(xp[row].astype(F32)).astype(BF)
    for side in (0, 1):
        for unit in range(rp.shape[1]):
            rp[side, unit] = gelu_value(rp[side, unit])
    halo_p.spread(xa, xa2)
    halo_e.wait_recv()
    halo_e.spread(xe, xe2)
    for k, (u, v) in enumerate(OFFSETS):
        block = window(xa, xa2, u, v, rows)
        act_t[pl.ds(k * block.shape[1], block.shape[1])] = block.T
        block = window(xe, xe2, u, v, rows)
        input_t[pl.ds(k * block.shape[1], block.shape[1])] = block.T

    @pl.loop(1, n_lead)
    def _(j):
        owner = (here.lead + j) % n_lead
        pltpu.make_async_remote_copy(
            src_ref=part.at[owner],
            dst_ref=parts_in.at[owner],
            send_sem=lead_send.at[owner],
            recv_sem=lead_recv.at[owner],
            device_id=(owner, here.lat, here.lon),
            device_id_type=MESH,
        ).wait_recv()

    parts_in[here.lead] = part[here.lead]
    for row in range(rows):
        total = parts_in[0, row].astype(F32)
        for a in range(1, n_lead):
            total += parts_in[a, row].astype(F32)
        x2[1 + row] = (total * slope_two[row]).astype(BF)
    halo_2.start_rows()
    halo_2.take_edges()
    halo_2.start_columns()

    def share_copy(stage, sent, taken, send_seat, recv_seat):
        return pltpu.make_async_remote_copy(
            src_ref=sent.at[send_seat],
            dst_ref=taken.at[recv_seat],
            send_sem=p1_send.at[stage, send_seat],
            recv_sem=p1_recv.at[stage, recv_seat],
            device_id=here.seat_device(send_seat),
            device_id_type=MESH,
        )

    def weight_grad(stage, turned, da, sent, taken):
        share = sent.shape[1]
        groups = UNIT
        per = seats // groups
        block = share * per

        @pl.loop(0, groups)
        def _(j):
            group = (here.seat // per + j) % groups
            begin = pl.multiple_of(group * block, block)
            product = matmul(turned[pl.ds(begin, block)], da, NN)
            for t in range(per):
                seat = group * per + t
                sent[seat] = product[t * share : (t + 1) * share].astype(BF)

                @pl.when(seat != here.seat)
                def _():
                    share_copy(stage, sent, taken, seat, here.seat).start()

    def plane_sum(stage, sent, taken):
        taken[here.seat] = sent[here.seat]

        @pl.loop(1, seats)
        def _(j):
            seat = (here.seat + j) % seats
            share_copy(stage, sent, taken, seat, seat).wait_recv()

        return lax.fori_loop(
            0,
            seats,
            lambda seat, total: total + taken[seat].astype(F32),
            jnp.zeros(taken.shape[1:], F32),
        )

    def final_copy(stage, sent, taken, lon, lead):
        return pltpu.make_async_remote_copy(
            src_ref=sent.at[lon],
            dst_ref=taken.at[here.z],
            send_sem=p2_send.at[stage, lon * n_lead + lead],
            recv_sem=p2_recv.at[stage, here.z],
            device_id=(lead, here.x * planes + target_z, lon),
            device_id_type=MESH,
        )

    def not_me(lon, lead):
        same = jnp.logical_and(lon == here.lon, lead == here.lead)
        return jnp.logical_not(jnp.logical_and(same, here.z == target_z))

    def spread_sums(stage, total, sent, taken):
        share = sent.shape[1]
        for lon in range(n_lon):
            sent[lon] = total[lon * share : (lon + 1) * share].astype(BF)

        @pl.loop(0, planes)
        def _(j):
            lon, lead = j // n_lead, j % n_lead

            @pl.when(not_me(lon, lead))
            def _():
                final_copy(stage, sent, taken, lon, lead).start()

        @pl.when(here.z == target_z)
        def _():
            taken[here.z] = sent[here.lon]

    def final_sum(stage, sent, taken, out):
        @pl.loop(0, planes)
        def _(z):
            @pl.when(jnp.logical_not(jnp.logical_and(own_feed, z == here.z)))
            def _():
                pltpu.make_async_remote_copy(
                    src_ref=sent.at[0],
                    dst_ref=taken.at[z],
                    send_sem=p2_send.at[stage, 0],
                    recv_sem=p2_recv.at[stage, z],
                    device_id=(feeder_lead, here.x * planes + z, feeder_lon),
                    device_id_type=MESH,
                ).wait_recv()

        total = taken[0].astype(F32)
        for z in range(1, planes):
            total += taken[z].astype(F32)
        out[...] = total * norm

    def tile(field):
        return field[pl.ds(1, rows)].reshape(cells, field.shape[-1])

    weight_grad(1, act_t, tile(x2), s1b, q1b)

    ready("w_two")
    halo_2.wait_recv()
    halo_2.spread(x2, x22)
    total = jnp.zeros((cells, w_two.shape[1]), F32)
    for k, (u, v) in enumerate(OFFSETS):
        total += matmul(window(x2, x22, -u, -v, rows), w_two[k], NT)
    da_first = total.reshape(slope_one.shape) * slope_one[...]
    x1[pl.ds(1, rows)] = da_first.astype(BF)
    halo_1.start_rows()
    halo_1.take_edges()
    halo_1.start_columns()
    weight_grad(0, input_t, tile(x1), s1a, q1a)

    spread_sums(1, plane_sum(1, s1b, q1b), s2b, q2b)

    ready("w_one")
    halo_1.wait_recv()
    halo_1.spread(x1, x12)
    total = jnp.zeros((cells, w_one.shape[1]), F32)
    for k, (u, v) in enumerate(OFFSETS):
        total += matmul(window(x1, x12, -u, -v, rows), w_one[k], NT)
    grad_stage[...] = total.astype(BF).reshape(grad_stage.shape)
    stores = [
        pltpu.make_async_copy(grad_stage.at[row], grad_out.at[:, row], load_sem.at[row])
        for row in range(rows)
    ]
    for copy in stores:
        copy.start()

    spread_sums(0, plane_sum(0, s1a, q1a), s2a, q2a)
    final_sum(1, s2b, q2b, second_out)
    final_sum(0, s2a, q2a, first_out)

    for copy in stores:
        copy.wait()
    for halo in (halo_h, halo_p, halo_e, halo_2, halo_1):
        halo.wait_send()

    @pl.loop(1, n_lead)
    def _(j):
        lead_copy((here.lead + j) % n_lead).wait_send()

    for stage, sent, taken in ((1, s1b, q1b), (0, s1a, q1a)):

        @pl.loop(1, seats)
        def _(j):
            seat = (here.seat + j) % seats
            share_copy(stage, sent, taken, seat, here.seat).wait_send()

    for stage, sent, taken in ((1, s2b, q2b), (0, s2a, q2a)):

        @pl.loop(0, planes)
        def _(j):
            lon, lead = j // n_lead, j % n_lead

            @pl.when(not_me(lon, lead))
            def _():
                final_copy(stage, sent, taken, lon, lead).wait_send()


def per_device(head_grads, head_weights, encoder_input, pre_first, pre_second, w_first, w_second):
    heads, batch_all, rows, cols, head_width = head_grads.shape
    samples, _, _, in_width = encoder_input.shape
    width = head_weights.shape[2]
    taps = len(OFFSETS)
    n_lead, n_lat, n_lon = lax.axis_size("lead"), lax.axis_size("lat"), lax.axis_size("lon")
    planes = n_lead * n_lon
    seats = n_lat
    lanes = heads * head_width
    cells = samples * rows * cols
    cells_total = cells * n_lead * n_lat * n_lon
    rows_two, rows_one = taps * width, taps * in_width
    share_two, share_one = rows_two // seats, rows_one // seats
    last_two, last_one = share_two // n_lon, share_one // n_lon

    def field(batch, lane):
        full = (rows + 2, batch, cols, lane)
        units = rows * batch // UNIT
        return (
            pltpu.VMEM(full, BF),
            pltpu.VMEM((2,) + full, BF),
            pltpu.VMEM((2, units, UNIT, lane), F32),
            pltpu.VMEM((2, units + 2, UNIT, lane), F32),
        )

    own = (rows, samples, cols, width)
    act_field = field(samples, width)
    scratch = [
        *field(batch_all, lanes),
        pltpu.VMEM((taps, width, lanes), BF),
        act_field[0], *act_field,
        *field(samples, in_width),
        *field(samples, width),
        *field(samples, width),
        pltpu.VMEM(own, BF),
        pltpu.VMEM(own, F32),
        pltpu.VMEM(own, F32),
        pltpu.VMEM(w_first.shape, BF),
        pltpu.VMEM(w_second.shape, BF),
        pltpu.VMEM((n_lead,) + own, BF),
        pltpu.VMEM((n_lead,) + own, BF),
        pltpu.VMEM((rows_two, cells), BF),
        pltpu.VMEM((rows_one, cells), BF),
        pltpu.VMEM((seats, share_two, width), BF),
        pltpu.VMEM((seats, share_two, width), BF),
        pltpu.VMEM((n_lon, last_two, width), BF),
        pltpu.VMEM((planes, last_two, width), BF),
        pltpu.VMEM((seats, share_one, width), BF),
        pltpu.VMEM((seats, share_one, width), BF),
        pltpu.VMEM((n_lon, last_one, width), BF),
        pltpu.VMEM((planes, last_one, width), BF),
        pltpu.VMEM((rows, samples, cols, in_width), BF),
        pltpu.SemaphoreType.DMA((64,)),
        pltpu.SemaphoreType.DMA((5, 16)),
        pltpu.SemaphoreType.DMA((5, 16)),
        pltpu.SemaphoreType.DMA((n_lead,)),
        pltpu.SemaphoreType.DMA((n_lead,)),
        pltpu.SemaphoreType.DMA((2, seats)),
        pltpu.SemaphoreType.DMA((2, seats)),
        pltpu.SemaphoreType.DMA((2, planes)),
        pltpu.SemaphoreType.DMA((2, planes)),
    ]
    anywhere = pl.BlockSpec(memory_space=pl.ANY)
    vmem = pl.BlockSpec(memory_space=pltpu.VMEM)
    input_grad, grad_first, grad_second = pl.pallas_call(
        functools.partial(kernel, 1.0 / math.sqrt(cells_total)),
        out_shape=(
            jax.ShapeDtypeStruct(encoder_input.shape, BF),
            jax.ShapeDtypeStruct((last_one, width), F32),
            jax.ShapeDtypeStruct((last_two, width), F32),
        ),
        in_specs=[anywhere] * 7,
        out_specs=(anywhere, vmem, vmem),
        scratch_shapes=scratch,
        compiler_params=pltpu.CompilerParams(
            collective_id=0, has_side_effects=True, vmem_limit_bytes=48 * 2**20
        ),
    )(head_grads, head_weights, encoder_input, pre_first, pre_second, w_first, w_second)
    return input_grad, grad_first.reshape(-1), grad_second.reshape(-1)


def solution(mesh):
    tile = P("lead", "lat", "lon", None)
    in_specs = (P("lead", None, "lat", "lon", None), P("lead", None, None, None), tile, tile, tile, P(), P())
    out_specs = (tile, P(("lat", "lon")), P(("lat", "lon")))
    return jax.shard_map(
        per_device, mesh=mesh, in_specs=in_specs, out_specs=out_specs, check_vma=False
    )
```

time: 844 us -> 120 us (0.14)
  the two profiles are of different devices: /device:TPU:2 before, /device:TPU:1 now
where the time goes in v1:
time: 120 us; the launch traced here: 118 us
  Pallas kernels  109 us (91%)
  local copies, waits for them, and re-layouts  9.12 us (8%)
    pallas_call x1, Pallas kernels, per_device(): pl.pallas_call(functools.partial(kernel, 1.0 / math.sqrt(cells_total)), o...  109 us
    unnamed x15, local copies, waits for them, and re-layouts  7.91 us

profile of v1, /device:TPU:1, one launch (start us, length us, event | category | flops | bytes accessed | tf_op | source)
XLA Modules:
  0.0 118.5 jit_solution(13590116494038439602)
XLA Ops:
  0.6 0.0 copy-start
  0.6 1.3 %copy-done = bf16[2,9,256,128]{3,2,1,0:T(8,128)(2,1)S(1)} copy-done((bf16[2,9,256,128]{3,2,1,0:T(8,128)(2,1)S(1)}, bf16[2,9,256,128]{3,2,1,0:T(8,128)(2,1)}, u32[]{:S(2)}) %copy-start) | copy-done | bytes 1179672
  1.9 0.0 copy-start.1
  1.9 1.3 %copy-done.1 = bf16[9,256,256]{2,1,0:T(8,128)(2,1)S(1)} copy-done((bf16[9,256,256]{2,1,0:T(8,128)(2,1)S(1)}, bf16[9,256,256]{2,1,0:T(8,128)(2,1)}, u32[]{:S(2)}) %copy-start.1) | copy-done | bytes 1179672
  3.2 0.0 copy-start.2
  3.2 1.1 copy-done.2
  4.2 0.0 copy-start.3
  4.2 1.0 copy-done.3
  5.3 0.0 copy-start.4
  5.3 0.9 copy-done.4
  6.2 0.0 copy-start.5
  6.2 0.9 copy-done.5
  7.1 0.0 copy-start.6
  7.1 0.8 copy-done.6
  7.9 108.7 %shard_map.94 = (bf16[2,4,32,128]{3,2,1,0:T(8,128)(2,1)S(1)}, f32[9,256]{1,0:T(8,128)S(1)}, f32[18,256]{1,0:T(8,128)S(1)}) custom-call(bf16[2,8,4,32,128]{4,3,2,1,0:T(8,128)(2,1)S(1)} %copy-done.3, bf16[2,9,256,128]{3,2,1,0:T(8,128)(2,1)S(1)} %copy-done, bf16[2,4,32,128]{3,2,1,0:T(8,128)(2,1)S(1)} %copy-done.6, bf16[2,4,32,256]{3,2,1,0:T(8,128)(2,1)S(1)} %copy-done.4, ...), custom_call_target="tpu_custom_call" | custom-call | tf_op jit(solution)/shard_map/pallas_call | solution.py:619
  116.6 0.6 reshape.12
  117.2 0.6 reshape.13
  117.8 0.6 copy.11
Async XLA Ops:
  0.6 1.3 %copy-start = (bf16[2,9,256,128]{3,2,1,0:T(8,128)(2,1)S(1)}, bf16[2,9,256,128]{3,2,1,0:T(8,128)(2,1)}, u32[]{:S(2)}) copy-start(bf16[2,9,256,128]{3,2,1,0:T(8,128)(2,1)} %head_w_hbm.1) | copy-start | bytes 3538948
  1.9 1.3 %copy-start.1 = (bf16[9,256,256]{2,1,0:T(8,128)(2,1)S(1)}, bf16[9,256,256]{2,1,0:T(8,128)(2,1)}, u32[]{:S(2)}) copy-start(bf16[9,256,256]{2,1,0:T(8,128)(2,1)} %w_second_hbm.1) | copy-start | bytes 3538948
  3.2 1.1 copy-start.2
  4.2 1.0 copy-start.3
  5.3 0.9 copy-start.4
  6.2 0.9 copy-start.5
  7.1 0.8 copy-start.6

commit v2 on v1

--- a/solution.py
+++ b/solution.py
@@ -40,18 +40,28 @@
         self.n_lead = lax.axis_size("lead")
         self.n_lat = lax.axis_size("lat")
         self.n_lon = lax.axis_size("lon")
-        self.planes = self.n_lead * self.n_lon
-        self.fold = self.n_lat // self.planes
-        self.x = self.lat // self.planes
+        self.planes = self.n_lat // 2
+        self.side = self.lat // self.planes
         self.z = self.lat % self.planes
-        self.seat = self.x * self.planes + self.lon * self.n_lead + self.lead
+        self.far = self.lead // 2
+        self.core = self.lead % 2
+        self.seats = 4 * self.n_lon
+        self.seat = self.seat_of(self.side, self.lon, self.far)
         self.has_low = self.lat > 0
         self.has_high = self.lat < self.n_lat - 1
 
+    def seat_of(self, side, lon, far):
+        return (side * self.n_lon + lon) * 2 + far
+
     def seat_device(self, seat):
-        rest = seat % self.planes
-        lat = (seat // self.planes) * self.planes + self.z
-        return (rest % self.n_lead, lat, rest // self.n_lead)
+        far, lon, side = seat % 2, seat // 2 % self.n_lon, seat // (2 * self.n_lon)
+        return (2 * far + self.core, side * self.planes + self.z, lon)
+
+    def lead_device(self, lead):
+        return (lead, self.lat, self.lon)
+
+    def plane_device(self, z):
+        return (self.lead, self.side * self.planes + z, self.lon)
 
     def near(self, rows, cols):
         return (self.lead, self.lat + rows, (self.lon + cols + self.n_lon) % self.n_lon)
@@ -201,18 +211,62 @@
     x1, x12, e1, r1,
     pre_two, slope_two, slope_one, w_one, w_two,
     part, parts_in,
-    act_t, input_t,
-    s1b, q1b, s2b, q2b, s1a, q1a, s2a, q2a,
+    act_t, input_t, act_mate, input_mate, da2_mate, da1_mate,
+    s1b, q1b, s2b, q2b, s3b, q3b, s1a, q1a, s2a, q2a, s3a, q3a,
     grad_stage,
-    load_sem, halo_send, halo_recv, lead_send, lead_recv,
-    p1_send, p1_recv, p2_send, p2_recv,
+    load_sem, halo_send, halo_recv, lead_send, lead_recv, mate_send, mate_recv,
+    p1_send, p1_recv, p2_send, p2_recv, p3_send, p3_recv,
 ):
     here = Place()
-    n_lead, planes, n_lon = here.n_lead, here.planes, here.n_lon
-    seats = here.fold * planes
+    n_lead, planes, n_lon, seats = here.n_lead, here.planes, here.n_lon, here.seats
+    half = planes // 2
     heads, batch_all, rows, cols, head_width = heads_hbm.shape
     samples = input_hbm.shape[0]
     cells = samples * rows * cols
+
+    barrier = pltpu.get_barrier_semaphore()
+
+    def greet(device):
+        pl.semaphore_signal(barrier, inc=1, device_id=device, device_id_type=MESH)
+
+    for has, step in ((here.has_low, -1), (here.has_high, 1)):
+
+        def greet_rows(step=step):
+            for col in (-1, 0, 1):
+                greet(here.near(step, col))
+
+        pl.when(has)(greet_rows)
+
+    for col in (-1, 1):
+        greet(here.near(0, col))
+    for j in range(1, n_lead):
+        greet(here.lead_device((here.lead + j) % n_lead))
+
+    @pl.loop(1, seats)
+    def _(j):
+        greet(here.seat_device((here.seat + j) % seats))
+
+    gathers = here.z // half == here.core
+    first_source = (here.z + here.far) % 2
+    first_target = here.core * half + first_source
+
+    @pl.when(gathers)
+    def _():
+        @pl.loop(0, half)
+        def _(j):
+            z = 2 * j + first_source
+
+            @pl.when(z != here.z)
+            def _():
+                greet(here.plane_device(z))
+
+    own_share = jnp.logical_and(gathers, here.far == 0)
+    greetings = (
+        2 + (n_lead - 1) + (seats - 1) + half // 2
+        + jnp.where(here.has_low, 3, 0)
+        + jnp.where(here.has_high, 3, 0)
+        - jnp.where(own_share, 1, 0)
+    )
 
     loads = {}
     count = 0
@@ -270,42 +324,6 @@
         x1, e1, r1, halo_send.at[4], halo_recv.at[4],
     )
 
-    barrier = pltpu.get_barrier_semaphore()
-
-    def greet(device):
-        pl.semaphore_signal(barrier, inc=1, device_id=device, device_id_type=MESH)
-
-    for has, step in ((here.has_low, -1), (here.has_high, 1)):
-
-        def greet_rows(step=step):
-            for col in (-1, 0, 1):
-                greet(here.near(step, col))
-
-        pl.when(has)(greet_rows)
-
-    @pl.loop(1, seats)
-    def _(j):
-        greet(here.seat_device((here.seat + j) % seats))
-
-    feeder_lon = here.z // n_lead
-    feeder_lead = here.z % n_lead
-    target_z = here.lon * n_lead + here.lead
-    own_feed = jnp.logical_and(here.lon == feeder_lon, here.lead == feeder_lead)
-
-    @pl.loop(0, planes)
-    def _(z):
-        @pl.when(jnp.logical_not(jnp.logical_and(own_feed, z == here.z)))
-        def _():
-            greet((feeder_lead, here.x * planes + z, feeder_lon))
-
-    greetings = (
-        seats - 1
-        + jnp.where(here.has_low, 3, 0)
-        + jnp.where(here.has_high, 3, 0)
-        + planes
-        - jnp.where(here.z == target_z, 1, 0)
-    )
-
     halo_h.clear()
     halo_p.clear()
     halo_e.clear()
@@ -371,6 +389,32 @@
         block = window(xe, xe2, u, v, rows)
         input_t[pl.ds(k * block.shape[1], block.shape[1])] = block.T
 
+    mate = here.lead + 1 - 2 * here.core
+
+    def mate_copy(number, source, target):
+        return pltpu.make_async_remote_copy(
+            src_ref=source,
+            dst_ref=target,
+            send_sem=mate_send.at[number],
+            recv_sem=mate_recv.at[number],
+            device_id=here.lead_device(mate),
+            device_id_type=MESH,
+        )
+
+    def turned_rows(turned, side, core):
+        block = turned.shape[0] // 4
+        return pl.ds(pl.multiple_of((2 * side + core) * block, block), block)
+
+    mates = [
+        mate_copy(2 * stage + side, turned.at[turned_rows(turned, side, 1 - here.core)], taken.at[side])
+        for stage, turned, taken in ((1, act_t, act_mate), (0, input_t, input_mate))
+        for side in (0, 1)
+    ]
+    mates.append(mate_copy(4, x2.at[pl.ds(1, rows)], da2_mate))
+    mates.append(mate_copy(5, x1.at[pl.ds(1, rows)], da1_mate))
+    for copy in mates[:4]:
+        copy.start()
+
     @pl.loop(1, n_lead)
     def _(j):
         owner = (here.lead + j) % n_lead
@@ -392,6 +436,7 @@
     halo_2.start_rows()
     halo_2.take_edges()
     halo_2.start_columns()
+    mates[4].start()
 
     def share_copy(stage, sent, taken, send_seat, recv_seat):
         return pltpu.make_async_remote_copy(
@@ -403,20 +448,27 @@
             device_id_type=MESH,
         )
 
-    def weight_grad(stage, turned, da, sent, taken):
-        share = sent.shape[1]
-        groups = UNIT
-        per = seats // groups
-        block = share * per
-
-        @pl.loop(0, groups)
+    def weight_grad(stage, turned, turned_mate, da, da_mate, sent, taken):
+        share = sent.shape[1] * 2 // half
+        da_mate = da_mate[...].reshape(da.shape)
+
+        @pl.loop(0, 2)
         def _(j):
-            group = (here.seat // per + j) % groups
-            begin = pl.multiple_of(group * block, block)
-            product = matmul(turned[pl.ds(begin, block)], da, NN)
-            for t in range(per):
-                seat = group * per + t
-                sent[seat] = product[t * share : (t + 1) * share].astype(BF)
+            side = (here.side + 1 + j) % 2
+            product = matmul(turned[turned_rows(turned, side, here.core)], da, NN)
+            product += matmul(turned_mate[side], da_mate, NN)
+            for lon in range(n_lon):
+                for odd in (0, 1):
+                    far = (odd + here.z) % 2
+                    seat = here.seat_of(side, lon, far)
+                    for t in range(half // 2):
+                        begin = ((2 * t + odd) * n_lon + lon) * share
+                        piece = product[begin : begin + share].astype(BF)
+                        sent[seat, t * share : (t + 1) * share] = piece
+
+            @pl.loop(0, 2 * n_lon)
+            def _(i):
+                seat = 2 * n_lon * side + (here.seat + 2 + i) % (2 * n_lon)
 
                 @pl.when(seat != here.seat)
                 def _():
@@ -430,67 +482,72 @@
             seat = (here.seat + j) % seats
             share_copy(stage, sent, taken, seat, seat).wait_recv()
 
-        return lax.fori_loop(
-            0,
-            seats,
-            lambda seat, total: total + taken[seat].astype(F32),
-            jnp.zeros(taken.shape[1:], F32),
-        )
-
-    def final_copy(stage, sent, taken, lon, lead):
+        total = taken[0].astype(F32)
+        for seat in range(1, seats):
+            total += taken[seat].astype(F32)
+        return total
+
+    def plane_copy(stage, sent, taken, t, slot, z):
         return pltpu.make_async_remote_copy(
-            src_ref=sent.at[lon],
-            dst_ref=taken.at[here.z],
-            send_sem=p2_send.at[stage, lon * n_lead + lead],
-            recv_sem=p2_recv.at[stage, here.z],
-            device_id=(lead, here.x * planes + target_z, lon),
+            src_ref=sent.at[t],
+            dst_ref=taken.at[slot],
+            send_sem=p2_send.at[stage, t],
+            recv_sem=p2_recv.at[stage, slot],
+            device_id=here.plane_device(z),
             device_id_type=MESH,
         )
 
-    def not_me(lon, lead):
-        same = jnp.logical_and(lon == here.lon, lead == here.lead)
-        return jnp.logical_not(jnp.logical_and(same, here.z == target_z))
-
-    def spread_sums(stage, total, sent, taken):
+    def send_planes(stage, total, sent, taken):
         share = sent.shape[1]
-        for lon in range(n_lon):
-            sent[lon] = total[lon * share : (lon + 1) * share].astype(BF)
-
-        @pl.loop(0, planes)
-        def _(j):
-            lon, lead = j // n_lead, j % n_lead
-
-            @pl.when(not_me(lon, lead))
-            def _():
-                final_copy(stage, sent, taken, lon, lead).start()
-
-        @pl.when(here.z == target_z)
+        for t in range(half // 2):
+            sent[t] = total[t * share : (t + 1) * share].astype(BF)
+        for t in range(half // 2):
+            z = first_target + 2 * t
+            copy = plane_copy(stage, sent, taken, t, here.z // 2, z)
+            pl.when(z != here.z)(copy.start)
+
+        @pl.when(own_share)
         def _():
-            taken[here.z] = sent[here.lon]
-
-    def final_sum(stage, sent, taken, out):
-        @pl.loop(0, planes)
-        def _(z):
-            @pl.when(jnp.logical_not(jnp.logical_and(own_feed, z == here.z)))
-            def _():
-                pltpu.make_async_remote_copy(
-                    src_ref=sent.at[0],
-                    dst_ref=taken.at[z],
-                    send_sem=p2_send.at[stage, 0],
-                    recv_sem=p2_recv.at[stage, z],
-                    device_id=(feeder_lead, here.x * planes + z, feeder_lon),
-                    device_id_type=MESH,
-                ).wait_recv()
-
-        total = taken[0].astype(F32)
-        for z in range(1, planes):
-            total += taken[z].astype(F32)
-        out[...] = total * norm
+            taken[here.z // 2] = sent[here.z % half // 2]
+
+    def last_copy(stage, sent, taken, lead, slot):
+        return pltpu.make_async_remote_copy(
+            src_ref=sent,
+            dst_ref=taken.at[slot],
+            send_sem=p3_send.at[stage, lead],
+            recv_sem=p3_recv.at[stage, slot],
+            device_id=here.lead_device(lead),
+            device_id_type=MESH,
+        )
+
+    def send_last(stage, sent, taken, last, last_taken):
+        @pl.when(gathers)
+        def _():
+            for j in range(half):
+                z = 2 * j + first_source
+                copy = plane_copy(stage, sent, taken, 0, j, z)
+                pl.when(z != here.z)(copy.wait_recv)
+            total = taken[0].astype(F32)
+            for j in range(1, half):
+                total += taken[j].astype(F32)
+            last[...] = total
+            for j in range(1, n_lead):
+                last_copy(stage, last, last_taken, (here.lead + j) % n_lead, here.far).start()
+            last_taken[here.far] = total
+
+    def final_sum(stage, last, last_taken, out):
+        for far in (0, 1):
+            source = 2 * far + here.z // half
+            copy = last_copy(stage, last, last_taken, source, far)
+            pl.when(source != here.lead)(copy.wait_recv)
+        out[...] = (last_taken[0] + last_taken[1]) * norm
 
     def tile(field):
         return field[pl.ds(1, rows)].reshape(cells, field.shape[-1])
 
-    weight_grad(1, act_t, tile(x2), s1b, q1b)
+    for number in (0, 1, 4):
+        mates[number].wait_recv()
+    weight_grad(1, act_t, act_mate, tile(x2), da2_mate, s1b, q1b)
 
     ready("w_two")
     halo_2.wait_recv()
@@ -503,9 +560,12 @@
     halo_1.start_rows()
     halo_1.take_edges()
     halo_1.start_columns()
-    weight_grad(0, input_t, tile(x1), s1a, q1a)
-
-    spread_sums(1, plane_sum(1, s1b, q1b), s2b, q2b)
+    mates[5].start()
+    for number in (2, 3, 5):
+        mates[number].wait_recv()
+    weight_grad(0, input_t, input_mate, tile(x1), da1_mate, s1a, q1a)
+
+    send_planes(1, plane_sum(1, s1b, q1b), s2b, q2b)
 
     ready("w_one")
     halo_1.wait_recv()
@@ -521,17 +581,19 @@
     for copy in stores:
         copy.start()
 
-    spread_sums(0, plane_sum(0, s1a, q1a), s2a, q2a)
-    final_sum(1, s2b, q2b, second_out)
-    final_sum(0, s2a, q2a, first_out)
-
+    send_planes(0, plane_sum(0, s1a, q1a), s2a, q2a)
+    send_last(1, s2b, q2b, s3b, q3b)
+    send_last(0, s2a, q2a, s3a, q3a)
+    final_sum(1, s3b, q3b, second_out)
+    final_sum(0, s3a, q3a, first_out)
     for copy in stores:
         copy.wait()
     for halo in (halo_h, halo_p, halo_e, halo_2, halo_1):
         halo.wait_send()
 
-    @pl.loop(1, n_lead)
-    def _(j):
+    for copy in mates:
+        copy.wait_send()
+    for j in range(1, n_lead):
         lead_copy((here.lead + j) % n_lead).wait_send()
 
     for stage, sent, taken in ((1, s1b, q1b), (0, s1a, q1a)):
@@ -542,14 +604,16 @@
             share_copy(stage, sent, taken, seat, here.seat).wait_send()
 
     for stage, sent, taken in ((1, s2b, q2b), (0, s2a, q2a)):
-
-        @pl.loop(0, planes)
-        def _(j):
-            lon, lead = j // n_lead, j % n_lead
-
-            @pl.when(not_me(lon, lead))
-            def _():
-                final_copy(stage, sent, taken, lon, lead).wait_send()
+        for t in range(half // 2):
+            z = first_target + 2 * t
+            copy = plane_copy(stage, sent, taken, t, here.z // 2, z)
+            pl.when(z != here.z)(copy.wait_send)
+
+    @pl.when(gathers)
+    def _():
+        for stage, last, last_taken in ((1, s3b, q3b), (0, s3a, q3a)):
+            for j in range(1, n_lead):
+                last_copy(stage, last, last_taken, (here.lead + j) % n_lead, here.far).wait_send()
 
 
 def per_device(head_grads, head_weights, encoder_input, pre_first, pre_second, w_first, w_second):
@@ -558,14 +622,13 @@
     width = head_weights.shape[2]
     taps = len(OFFSETS)
     n_lead, n_lat, n_lon = lax.axis_size("lead"), lax.axis_size("lat"), lax.axis_size("lon")
-    planes = n_lead * n_lon
-    seats = n_lat
+    half = n_lat // 4
+    seats = 4 * n_lon
     lanes = heads * head_width
     cells = samples * rows * cols
     cells_total = cells * n_lead * n_lat * n_lon
     rows_two, rows_one = taps * width, taps * in_width
-    share_two, share_one = rows_two // seats, rows_one // seats
-    last_two, last_one = share_two // n_lon, share_one // n_lon
+    last_two, last_one = rows_two // (n_lat * n_lon), rows_one // (n_lat * n_lon)
 
     def field(batch, lane):
         full = (rows + 2, batch, cols, lane)
@@ -575,6 +638,16 @@
             pltpu.VMEM((2,) + full, BF),
             pltpu.VMEM((2, units, UNIT, lane), F32),
             pltpu.VMEM((2, units + 2, UNIT, lane), F32),
+        )
+
+    def reduce_buffers(share):
+        return (
+            pltpu.VMEM((seats, share * half // 2, width), BF),
+            pltpu.VMEM((seats, share * half // 2, width), BF),
+            pltpu.VMEM((half // 2, share, width), BF),
+            pltpu.VMEM((half, share, width), BF),
+            pltpu.VMEM((share, width), F32),
+            pltpu.VMEM((2, share, width), F32),
         )
 
     own = (rows, samples, cols, width)
@@ -595,24 +668,26 @@
         pltpu.VMEM((n_lead,) + own, BF),
         pltpu.VMEM((rows_two, cells), BF),
         pltpu.VMEM((rows_one, cells), BF),
-        pltpu.VMEM((seats, share_two, width), BF),
-        pltpu.VMEM((seats, share_two, width), BF),
-        pltpu.VMEM((n_lon, last_two, width), BF),
-        pltpu.VMEM((planes, last_two, width), BF),
-        pltpu.VMEM((seats, share_one, width), BF),
-        pltpu.VMEM((seats, share_one, width), BF),
-        pltpu.VMEM((n_lon, last_one, width), BF),
-        pltpu.VMEM((planes, last_one, width), BF),
+        pltpu.VMEM((2, rows_two // 4, cells), BF),
+        pltpu.VMEM((2, rows_one // 4, cells), BF),
+        pltpu.VMEM(own, BF),
+        pltpu.VMEM(own, BF),
+        *reduce_buffers(last_two),
+        *reduce_buffers(last_one),
         pltpu.VMEM((rows, samples, cols, in_width), BF),
         pltpu.SemaphoreType.DMA((64,)),
         pltpu.SemaphoreType.DMA((5, 16)),
         pltpu.SemaphoreType.DMA((5, 16)),
         pltpu.SemaphoreType.DMA((n_lead,)),
         pltpu.SemaphoreType.DMA((n_lead,)),
+        pltpu.SemaphoreType.DMA((6,)),
+        pltpu.SemaphoreType.DMA((6,)),
         pltpu.SemaphoreType.DMA((2, seats)),
         pltpu.SemaphoreType.DMA((2, seats)),
-        pltpu.SemaphoreType.DMA((2, planes)),
-        pltpu.SemaphoreType.DMA((2, planes)),
+        pltpu.SemaphoreType.DMA((2, half // 2)),
+        pltpu.SemaphoreType.DMA((2, half)),
+        pltpu.SemaphoreType.DMA((2, n_lead)),
+        pltpu.SemaphoreType.DMA((2, 2)),
     ]
     anywhere = pl.BlockSpec(memory_space=pl.ANY)
     vmem = pl.BlockSpec(memory_space=pltpu.VMEM)

time: 120 us -> 69.7 us (0.58)
  Pallas kernels: 109 us -> 59.5 us
    pallas_call x1, Pallas kernels: 109 us -> 59.5 us  [per_device(): pl.pallas_call(functools.partial(kernel, 1.0 / math.sqrt(cells_total)), o...]
where the time goes in v2:
time: 69.7 us; the launch traced here: 69.3 us
  Pallas kernels  59.5 us (85%)
  local copies, waits for them, and re-layouts  9.12 us (13%)
    pallas_call x1, Pallas kernels, per_device(): pl.pallas_call(functools.partial(kernel, 1.0 / math.sqrt(cells_total)), o...  59.5 us
    unnamed x15, local copies, waits for them, and re-layouts  7.91 us

profile of v2, /device:TPU:1, one launch (start us, length us, event | category | flops | bytes accessed | tf_op | source)
XLA Modules:
  0.0 69.3 jit_solution(13824803497637922164)
XLA Ops:
  0.6 0.0 copy-start
  0.6 1.3 %copy-done = bf16[2,9,256,128]{3,2,1,0:T(8,128)(2,1)S(1)} copy-done((bf16[2,9,256,128]{3,2,1,0:T(8,128)(2,1)S(1)}, bf16[2,9,256,128]{3,2,1,0:T(8,128)(2,1)}, u32[]{:S(2)}) %copy-start) | copy-done | bytes 1179672
  1.9 0.0 copy-start.1
  1.9 1.3 %copy-done.1 = bf16[9,256,256]{2,1,0:T(8,128)(2,1)S(1)} copy-done((bf16[9,256,256]{2,1,0:T(8,128)(2,1)S(1)}, bf16[9,256,256]{2,1,0:T(8,128)(2,1)}, u32[]{:S(2)}) %copy-start.1) | copy-done | bytes 1179672
  3.2 0.0 copy-start.2
  3.2 1.1 %copy-done.2 = bf16[9,128,256]{2,1,0:T(8,128)(2,1)S(1)} copy-done((bf16[9,128,256]{2,1,0:T(8,128)(2,1)S(1)}, bf16[9,128,256]{2,1,0:T(8,128)(2,1)}, u32[]{:S(2)}) %copy-start.2) | copy-done | bytes 589848
  4.2 0.0 copy-start.3
  4.2 1.0 %copy-done.3 = bf16[2,8,4,32,128]{4,3,2,1,0:T(8,128)(2,1)S(1)} copy-done((bf16[2,8,4,32,128]{4,3,2,1,0:T(8,128)(2,1)S(1)}, bf16[2,8,4,32,128]{4,3,2,1,0:T(8,128)(2,1)}, u32[]{:S(2)}) %copy-start.3) | copy-done | bytes 524312
  5.3 0.0 copy-start.4
  5.3 0.9 %copy-done.4 = bf16[2,4,32,256]{3,2,1,0:T(8,128)(2,1)S(1)} copy-done((bf16[2,4,32,256]{3,2,1,0:T(8,128)(2,1)S(1)}, bf16[2,4,32,256]{3,2,1,0:T(8,128)(2,1)}, u32[]{:S(2)}) %copy-start.4) | copy-done | bytes 131096
  6.2 0.0 copy-start.5
  6.2 0.9 %copy-done.5 = bf16[2,4,32,256]{3,2,1,0:T(8,128)(2,1)S(1)} copy-done((bf16[2,4,32,256]{3,2,1,0:T(8,128)(2,1)S(1)}, bf16[2,4,32,256]{3,2,1,0:T(8,128)(2,1)}, u32[]{:S(2)}) %copy-start.5) | copy-done | bytes 131096
  7.1 0.0 copy-start.6
  7.1 0.8 %copy-done.6 = bf16[2,4,32,128]{3,2,1,0:T(8,128)(2,1)S(1)} copy-done((bf16[2,4,32,128]{3,2,1,0:T(8,128)(2,1)S(1)}, bf16[2,4,32,128]{3,2,1,0:T(8,128)(2,1)}, u32[]{:S(2)}) %copy-start.6) | copy-done | bytes 65560
  7.9 59.5 %shard_map.94 = (bf16[2,4,32,128]{3,2,1,0:T(8,128)(2,1)S(1)}, f32[9,256]{1,0:T(8,128)S(1)}, f32[18,256]{1,0:T(8,128)S(1)}) custom-call(bf16[2,8,4,32,128]{4,3,2,1,0:T(8,128)(2,1)S(1)} %copy-done.3, bf16[2,9,256,128]{3,2,1,0:T(8,128)(2,1)S(1)} %copy-done, bf16[2,4,32,128]{3,2,1,0:T(8,128)(2,1)S(1)} %copy-done.6, bf16[2,4,32,256]{3,2,1,0:T(8,128)(2,1)S(1)} %copy-done.4, ...), custom_call_target="tpu_custom_call" | custom-call | tf_op jit(solution)/shard_map/pallas_call | solution.py:694
  67.5 0.6 reshape.12
  68.1 0.6 reshape.13
  68.7 0.6 copy.11
Async XLA Ops:
  0.6 1.3 %copy-start = (bf16[2,9,256,128]{3,2,1,0:T(8,128)(2,1)S(1)}, bf16[2,9,256,128]{3,2,1,0:T(8,128)(2,1)}, u32[]{:S(2)}) copy-start(bf16[2,9,256,128]{3,2,1,0:T(8,128)(2,1)} %head_w_hbm.1) | copy-start | bytes 3538948
  1.9 1.3 %copy-start.1 = (bf16[9,256,256]{2,1,0:T(8,128)(2,1)S(1)}, bf16[9,256,256]{2,1,0:T(8,128)(2,1)}, u32[]{:S(2)}) copy-start(bf16[9,256,256]{2,1,0:T(8,128)(2,1)} %w_second_hbm.1) | copy-start | bytes 3538948
  3.2 1.1 %copy-start.2 = (bf16[9,128,256]{2,1,0:T(8,128)(2,1)S(1)}, bf16[9,128,256]{2,1,0:T(8,128)(2,1)}, u32[]{:S(2)}) copy-start(bf16[9,128,256]{2,1,0:T(8,128)(2,1)} %w_first_hbm.1) | copy-start | bytes 1769476
  4.2 1.0 %copy-start.3 = (bf16[2,8,4,32,128]{4,3,2,1,0:T(8,128)(2,1)S(1)}, bf16[2,8,4,32,128]{4,3,2,1,0:T(8,128)(2,1)}, u32[]{:S(2)}) copy-start(bf16[2,8,4,32,128]{4,3,2,1,0:T(8,128)(2,1)} %heads_hbm.1) | copy-start | bytes 1572868
  5.3 0.9 %copy-start.4 = (bf16[2,4,32,256]{3,2,1,0:T(8,128)(2,1)S(1)}, bf16[2,4,32,256]{3,2,1,0:T(8,128)(2,1)}, u32[]{:S(2)}) copy-start(bf16[2,4,32,256]{3,2,1,0:T(8,128)(2,1)} %first_hbm.1) | copy-start | bytes 393220
  6.2 0.9 %copy-start.5 = (bf16[2,4,32,256]{3,2,1,0:T(8,128)(2,1)S(1)}, bf16[2,4,32,256]{3,2,1,0:T(8,128)(2,1)}, u32[]{:S(2)}) copy-start(bf16[2,4,32,256]{3,2,1,0:T(8,128)(2,1)} %second_hbm.1) | copy-start | bytes 393220
  7.1 0.8 %copy-start.6 = (bf16[2,4,32,128]{3,2,1,0:T(8,128)(2,1)S(1)}, bf16[2,4,32,128]{3,2,1,0:T(8,128)(2,1)}, u32[]{:S(2)}) copy-start(bf16[2,4,32,128]{3,2,1,0:T(8,128)(2,1)} %input_hbm.1) | copy-start | bytes 196612

commit v3 on v2

--- a/solution.py
+++ b/solution.py
@@ -129,8 +129,19 @@
     def start_columns(self):
         self.run(self.copies[self.row_count :], 0, "start")
 
+    def wait_columns(self):
+        self.run(self.copies[self.row_count : self.row_count + 2], 1, "wait_recv")
+
+    def wait_side(self, high):
+        each = self.row_count // 2
+        corner = self.row_count + 2 + 2 * high
+        items = self.copies[high * each : (high + 1) * each] + self.copies[corner : corner + 2]
+        self.run(items, 1, "wait_recv")
+
     def wait_recv(self):
-        self.run(self.copies, 1, "wait_recv")
+        self.wait_columns()
+        self.wait_side(0)
+        self.wait_side(1)
 
     def wait_send(self):
         self.run(self.copies, 0, "wait_send")
@@ -173,8 +184,8 @@
             unit = unit + 1
         return self.ring[side, unit, sub : sub + 1]
 
-    def spread(self, base, out):
-        for ext in range(self.rows + 2):
+    def spread(self, base, out, rows=None):
+        for ext in range(self.rows + 2) if rows is None else rows:
             for b in range(self.batch):
                 block = base[ext, b].astype(F32)
                 column = lax.broadcasted_iota(jnp.int32, block.shape, 0)
@@ -190,8 +201,8 @@
                 out[1, ext, b] = ahead.astype(BF)
 
 
-def window(base, spread, step_row, step_col, rows, batch=None):
-    row = pl.ds(1 + step_row, rows)
+def window(base, spread, step_row, step_col, rows, batch=None, first=0):
+    row = pl.ds(1 + first + step_row, rows)
     if step_col == 0:
         view = base[row] if batch is None else base[row, batch]
     else:
@@ -329,10 +340,10 @@
     halo_e.clear()
     halo_2.clear()
     halo_1.clear()
+    pl.semaphore_wait(barrier, greetings)
+    halo_h.start_rows()
     ready("heads")
     halo_h.take_edges()
-    pl.semaphore_wait(barrier, greetings)
-    halo_h.start_rows()
     halo_h.start_columns()
     ready("first")
     halo_p.take_edges()
@@ -344,31 +355,46 @@
     halo_e.start_columns()
     ready("head_w")
 
-    halo_h.wait_recv()
-    halo_h.spread(xh, xh2)
-
-    def lead_copy(owner):
+    pieces = (pl.ds(1, rows - 2), pl.ds(0, 1), pl.ds(rows - 1, 1))
+
+    def lead_copy(source, owner, piece):
         return pltpu.make_async_remote_copy(
-            src_ref=part.at[owner],
-            dst_ref=parts_in.at[here.lead],
-            send_sem=lead_send.at[owner],
-            recv_sem=lead_recv.at[here.lead],
-            device_id=(owner, here.lat, here.lon),
+            src_ref=part.at[owner, pieces[piece]],
+            dst_ref=parts_in.at[source, pieces[piece]],
+            send_sem=lead_send.at[owner, piece],
+            recv_sem=lead_recv.at[source, piece],
+            device_id=here.lead_device(owner),
             device_id_type=MESH,
         )
 
-    @pl.loop(0, n_lead)
+    def convolve(first, count, batch):
+        total = None
+        for k, (u, v) in enumerate(OFFSETS):
+            term = matmul(window(xh, xh2, -u, -v, count, batch, first), head_w[k], NT)
+            total = term if total is None else total + term
+        return total.astype(BF)
+
+    halo_h.wait_columns()
+    halo_h.spread(xh, xh2, range(1, rows + 1))
+    @pl.loop(0, 2)
     def _(j):
-        owner = (here.lead + n_lead - 1 - j) % n_lead
-        batch = pl.ds(owner * samples, samples)
-        total = jnp.zeros((cells, head_w.shape[1]), F32)
-        for k, (u, v) in enumerate(OFFSETS):
-            total += matmul(window(xh, xh2, -u, -v, rows, batch), head_w[k], NT)
-        part[owner] = total.astype(BF).reshape(part.shape[1:])
-
-        @pl.when(owner != here.lead)
-        def _():
-            lead_copy(owner).start()
+        far = (here.far + 1 + j) % 2
+        block = convolve(1, rows - 2, pl.ds(far * 2 * samples, 2 * samples))
+        block = block.reshape((rows - 2, 2 * samples) + part.shape[3:])
+        for core in (0, 1):
+            owner = 2 * far + core
+            part[owner, pieces[0]] = block[:, core * samples : (core + 1) * samples]
+            copy = lead_copy(here.lead, owner, 0)
+            pl.when(owner != here.lead)(copy.start)
+
+    for high in (0, 1):
+        halo_h.wait_side(high)
+        halo_h.spread(xh, xh2, [(rows + 1) * high])
+        block = convolve((rows - 1) * high, 1, pl.ds(0, batch_all)).reshape((batch_all,) + part.shape[3:])
+        for owner in range(n_lead):
+            part[owner, (rows - 1) * high] = block[owner * samples : (owner + 1) * samples]
+        for j in (2, 3, 1):
+            lead_copy(here.lead, (here.lead + j) % n_lead, 1 + high).start()
 
     ready("second")
     for row in range(rows):
@@ -415,18 +441,10 @@
     for copy in mates[:4]:
         copy.start()
 
-    @pl.loop(1, n_lead)
-    def _(j):
-        owner = (here.lead + j) % n_lead
-        pltpu.make_async_remote_copy(
-            src_ref=part.at[owner],
-            dst_ref=parts_in.at[owner],
-            send_sem=lead_send.at[owner],
-            recv_sem=lead_recv.at[owner],
-            device_id=(owner, here.lat, here.lon),
-            device_id_type=MESH,
-        ).wait_recv()
-
+    for j in range(1, n_lead):
+        source = (here.lead + j) % n_lead
+        for piece in range(len(pieces)):
+            lead_copy(source, source, piece).wait_recv()
     parts_in[here.lead] = part[here.lead]
     for row in range(rows):
         total = parts_in[0, row].astype(F32)
@@ -448,15 +466,20 @@
             device_id_type=MESH,
         )
 
-    def weight_grad(stage, turned, turned_mate, da, da_mate, sent, taken):
+    def weight_grad(stage, turned, turned_mate, da, da_mate, sent, taken, waits):
         share = sent.shape[1] * 2 // half
-        da_mate = da_mate[...].reshape(da.shape)
 
         @pl.loop(0, 2)
         def _(j):
             side = (here.side + 1 + j) % 2
             product = matmul(turned[turned_rows(turned, side, here.core)], da, NN)
-            product += matmul(turned_mate[side], da_mate, NN)
+
+            @pl.when(j == 0)
+            def _():
+                for number in waits:
+                    mates[number].wait_recv()
+
+            product += matmul(turned_mate[side], da_mate[...].reshape(da.shape), NN)
             for lon in range(n_lon):
                 for odd in (0, 1):
                     far = (odd + here.z) % 2
@@ -545,9 +568,7 @@
     def tile(field):
         return field[pl.ds(1, rows)].reshape(cells, field.shape[-1])
 
-    for number in (0, 1, 4):
-        mates[number].wait_recv()
-    weight_grad(1, act_t, act_mate, tile(x2), da2_mate, s1b, q1b)
+    weight_grad(1, act_t, act_mate, tile(x2), da2_mate, s1b, q1b, (0, 1, 4))
 
     ready("w_two")
     halo_2.wait_recv()
@@ -561,9 +582,7 @@
     halo_1.take_edges()
     halo_1.start_columns()
     mates[5].start()
-    for number in (2, 3, 5):
-        mates[number].wait_recv()
-    weight_grad(0, input_t, input_mate, tile(x1), da1_mate, s1a, q1a)
+    weight_grad(0, input_t, input_mate, tile(x1), da1_mate, s1a, q1a, (2, 3, 5))
 
     send_planes(1, plane_sum(1, s1b, q1b), s2b, q2b)
 
@@ -584,8 +603,6 @@
     send_planes(0, plane_sum(0, s1a, q1a), s2a, q2a)
     send_last(1, s2b, q2b, s3b, q3b)
     send_last(0, s2a, q2a, s3a, q3a)
-    final_sum(1, s3b, q3b, second_out)
-    final_sum(0, s3a, q3a, first_out)
     for copy in stores:
         copy.wait()
     for halo in (halo_h, halo_p, halo_e, halo_2, halo_1):
@@ -594,7 +611,8 @@
     for copy in mates:
         copy.wait_send()
     for j in range(1, n_lead):
-        lead_copy((here.lead + j) % n_lead).wait_send()
+        for piece in range(len(pieces)):
+            lead_copy(here.lead, (here.lead + j) % n_lead, piece).wait_send()
 
     for stage, sent, taken in ((1, s1b, q1b), (0, s1a, q1a)):
 
@@ -603,6 +621,8 @@
             seat = (here.seat + j) % seats
             share_copy(stage, sent, taken, seat, here.seat).wait_send()
 
+    final_sum(1, s3b, q3b, second_out)
+    final_sum(0, s3a, q3a, first_out)
     for stage, sent, taken in ((1, s2b, q2b), (0, s2a, q2a)):
         for t in range(half // 2):
             z = first_target + 2 * t
@@ -678,8 +698,8 @@
         pltpu.SemaphoreType.DMA((64,)),
         pltpu.SemaphoreType.DMA((5, 16)),
         pltpu.SemaphoreType.DMA((5, 16)),
-        pltpu.SemaphoreType.DMA((n_lead,)),
-        pltpu.SemaphoreType.DMA((n_lead,)),
+        pltpu.SemaphoreType.DMA((n_lead, 3)),
+        pltpu.SemaphoreType.DMA((n_lead, 3)),
         pltpu.SemaphoreType.DMA((6,)),
         pltpu.SemaphoreType.DMA((6,)),
         pltpu.SemaphoreType.DMA((2, seats)),
@@ -702,7 +722,7 @@
         out_specs=(anywhere, vmem, vmem),
         scratch_shapes=scratch,
         compiler_params=pltpu.CompilerParams(
-            collective_id=0, has_side_effects=True, vmem_limit_bytes=48 * 2**20
+            collective_id=0, has_side_effects=True, vmem_limit_bytes=56 * 2**20
         ),
     )(head_grads, head_weights, encoder_input, pre_first, pre_second, w_first, w_second)
     return input_grad, grad_first.reshape(-1), grad_second.reshape(-1)

time: 69.7 us -> 62.4 us (0.90)
  local copies, waits for them, and re-layouts: 9.12 us -> 4.14 us
  Pallas kernels: 59.5 us -> 57 us
    unnamed x15 -> x1, local copies, waits for them, and re-layouts: 7.91 us -> 1.47 us
    pallas_call x1, Pallas kernels: 59.5 us -> 57 us  [per_device(): pl.pallas_call(functools.partial(kernel, 1.0 / math.sqrt(cells_total)), o...]
    reshape x2, local copies, waits for them, and re-layouts: 1.21 us -> 2.66 us  [per_device(): return (input_grad, grad_first.reshape(-1), grad_second.reshape(-1))]
where the time goes in v3:
time: 62.4 us; the launch traced here: 61.8 us
  Pallas kernels  57 us (91%)
  local copies, waits for them, and re-layouts  4.14 us (7%)
  between operations  0.64 us (1%)
    pallas_call x1, Pallas kernels, per_device(): pl.pallas_call(functools.partial(kernel, 1.0 / math.sqrt(cells_total)), o...  57 us
    reshape x2, local copies, waits for them, and re-layouts, per_device(): return (input_grad, grad_first.reshape(-1), grad_second.reshape(-1))  2.66 us
    unnamed x1, local copies, waits for them, and re-layouts  1.47 us

profile of v3, /device:TPU:1, one launch (start us, length us, event | category | flops | bytes accessed | tf_op | source)
XLA Modules:
  0.0 61.8 jit_solution(17010241350808466396)
XLA Ops:
  0.6 57.0 %shard_map.94 = (bf16[2,4,32,128]{3,2,1,0:T(8,128)(2,1)}, f32[9,256]{1,0:T(8,128)}, f32[18,256]{1,0:T(8,128)}) custom-call(bf16[2,8,4,32,128]{4,3,2,1,0:T(8,128)(2,1)} %heads_hbm.1, bf16[2,9,256,128]{3,2,1,0:T(8,128)(2,1)} %head_w_hbm.1, bf16[2,4,32,128]{3,2,1,0:T(8,128)(2,1)} %input_hbm.1, bf16[2,4,32,256]{3,2,1,0:T(8,128)(2,1)} %first_hbm.1, ...), custom_call_target="tpu_custom_call" | custom-call | tf_op jit(solution)/shard_map/pallas_call | solution.py:714
  57.6 1.3 %reshape.12 = f32[2304]{0:T(1024)} reshape(f32[9,256]{1,0:T(8,128)} %get-tuple-element.7) | data formatting | bytes 18432 | tf_op jit(solution)/shard_map/reshape | solution.py:728
  59.0 1.3 %reshape.13 = f32[4608]{0:T(1024)} reshape(f32[18,256]{1,0:T(8,128)} %get-tuple-element.8) | data formatting | bytes 36864 | tf_op jit(solution)/shard_map/reshape | solution.py:728
  60.3 1.5 %copy.11 = bf16[2,4,32,128]{3,2,1,0:T(8,128)(2,1)} copy(bf16[2,4,32,128]{3,2,1,0:T(8,128)(2,1)} %get-tuple-element.12) | data formatting | bytes 131072

commit v4 on v3

--- a/solution.py
+++ b/solution.py
@@ -75,68 +75,74 @@
         self.batch = field.shape[1]
         self.cols = field.shape[2]
         copies = []
-        slot = 0
         for high in (0, 1):
             step = 1 if high == 0 else -1
             sends = here.has_high if high == 0 else here.has_low
-            takes = here.has_low if high == 0 else here.has_high
             for source, target in zip(rows_out[high], rows_in[high]):
-                copies.append((sends, takes, source, target, here.near(step, 0), slot))
-                slot += 1
-        self.row_count = slot
+                copies.append((sends, source, target, here.near(step, 0), 1 + high))
+        self.row_count = len(copies)
         body = pl.ds(1, self.units)
         for right in (0, 1):
             step = 1 if right == 0 else -1
-            source = edge.at[1 - right]
-            copies.append((None, None, source, ring.at[right, body], here.near(0, step), slot))
-            slot += 1
+            copies.append((None, edge.at[1 - right], ring.at[right, body], here.near(0, step), 0))
         for high in (0, 1):
             for right in (0, 1):
                 row_step = 1 if high == 0 else -1
                 col_step = 1 if right == 0 else -1
                 sends = here.has_high if high == 0 else here.has_low
-                takes = here.has_low if high == 0 else here.has_high
                 source = edge.at[1 - right, self.units - 1 if high == 0 else 0]
                 target = ring.at[right, 0 if high == 0 else self.units + 1]
-                copies.append((sends, takes, source, target, here.near(row_step, col_step), slot))
-                slot += 1
+                copies.append((sends, source, target, here.near(row_step, col_step), 3 + high))
+
+        def remote(source, target, device, number):
+            return pltpu.make_async_remote_copy(
+                src_ref=source,
+                dst_ref=target,
+                send_sem=send.at[number],
+                recv_sem=recv.at[number],
+                device_id=device,
+                device_id_type=MESH,
+            )
+
         self.copies = [
-            (
-                sends,
-                takes,
-                pltpu.make_async_remote_copy(
-                    src_ref=source,
-                    dst_ref=target,
-                    send_sem=send.at[number],
-                    recv_sem=recv.at[number],
-                    device_id=device,
-                    device_id_type=MESH,
-                ),
-            )
-            for sends, takes, source, target, device, number in copies
+            (sends, remote(source, target, device, number))
+            for sends, source, target, device, number in copies
         ]
-
-    def run(self, items, which, name):
-        for item in items:
-            if item[which] is None:
-                getattr(item[2], name)()
+        far_rows = (0, self.rows + 1)
+        far_units = (0, self.units + 1)
+        self.columns = remote(edge, ring.at[:, body], here.near(0, 1), 0)
+        self.row_groups = [
+            remote(field.at[far_rows[high]], field.at[far_rows[high]], here.near(0, 1), 1 + high)
+            for high in (0, 1)
+        ]
+        self.corner_groups = [
+            remote(edge.at[:, 0], ring.at[:, far_units[high]], here.near(0, 1), 3 + high)
+            for high in (0, 1)
+        ]
+
+    def start(self, items):
+        for sends, copy in items:
+            if sends is None:
+                copy.start()
             else:
-                pl.when(item[which])(getattr(item[2], name))
+                pl.when(sends)(copy.start)
 
     def start_rows(self):
-        self.run(self.copies[: self.row_count], 0, "start")
+        self.start(self.copies[: self.row_count])
 
     def start_columns(self):
-        self.run(self.copies[self.row_count :], 0, "start")
+        self.start(self.copies[self.row_count :])
 
     def wait_columns(self):
-        self.run(self.copies[self.row_count : self.row_count + 2], 1, "wait_recv")
+        self.columns.wait_recv()
 
     def wait_side(self, high):
-        each = self.row_count // 2
-        corner = self.row_count + 2 + 2 * high
-        items = self.copies[high * each : (high + 1) * each] + self.copies[corner : corner + 2]
-        self.run(items, 1, "wait_recv")
+        takes = self.here.has_high if high else self.here.has_low
+
+        @pl.when(takes)
+        def _():
+            self.row_groups[high].wait_recv()
+            self.corner_groups[high].wait_recv()
 
     def wait_recv(self):
         self.wait_columns()
@@ -144,7 +150,14 @@
         self.wait_side(1)
 
     def wait_send(self):
-        self.run(self.copies, 0, "wait_send")
+        self.columns.wait_send()
+        for high in (0, 1):
+            sends = self.here.has_low if high else self.here.has_high
+
+            @pl.when(sends)
+            def _(high=high):
+                self.row_groups[high].wait_send()
+                self.corner_groups[high].wait_send()
 
     def clear(self):
         def low():
@@ -279,15 +292,15 @@
         - jnp.where(own_share, 1, 0)
     )
 
-    loads = {}
-    count = 0
+    names = ("heads", "first", "input", "head_w", "second", "w_two", "w_one", "out")
+    body = pl.ds(1, rows)
+    whole = {
+        "heads": xh.at[body], "first": xp.at[body], "input": xe.at[body], "head_w": head_w,
+        "second": pre_two, "w_two": w_two, "w_one": w_one, "out": grad_stage,
+    }
 
     def load(key, source, target):
-        nonlocal count
-        copy = pltpu.make_async_copy(source, target, load_sem.at[count])
-        copy.start()
-        loads.setdefault(key, []).append(copy)
-        count += 1
+        pltpu.make_async_copy(source, target, load_sem.at[names.index(key)]).start()
 
     for row in range(rows):
         for h in range(heads):
@@ -304,8 +317,7 @@
     load("w_one", w_first_hbm, w_one)
 
     def ready(key):
-        for copy in loads[key]:
-            copy.wait()
+        pltpu.make_async_copy(whole[key], whole[key], load_sem.at[names.index(key)]).wait()
 
     lane = [pl.ds(h * head_width, head_width) for h in range(heads)]
     halo_h = Halo(
@@ -357,12 +369,22 @@
 
     pieces = (pl.ds(1, rows - 2), pl.ds(0, 1), pl.ds(rows - 1, 1))
 
+    others = pl.ds(0, n_lead - 1)
+    lead_group = pltpu.make_async_remote_copy(
+        src_ref=part.at[others],
+        dst_ref=parts_in.at[others],
+        send_sem=lead_send.at[0],
+        recv_sem=lead_recv.at[0],
+        device_id=here.near(0, 1),
+        device_id_type=MESH,
+    )
+
     def lead_copy(source, owner, piece):
         return pltpu.make_async_remote_copy(
             src_ref=part.at[owner, pieces[piece]],
             dst_ref=parts_in.at[source, pieces[piece]],
-            send_sem=lead_send.at[owner, piece],
-            recv_sem=lead_recv.at[source, piece],
+            send_sem=lead_send.at[0],
+            recv_sem=lead_recv.at[0],
             device_id=here.lead_device(owner),
             device_id_type=MESH,
         )
@@ -431,20 +453,18 @@
         block = turned.shape[0] // 4
         return pl.ds(pl.multiple_of((2 * side + core) * block, block), block)
 
+    for stage, turned, taken in ((1, act_t, act_mate), (0, input_t, input_mate)):
+        for side in (0, 1):
+            rows_there = turned_rows(turned, side, 1 - here.core)
+            mate_copy(stage, turned.at[rows_there], taken.at[side]).start()
     mates = [
-        mate_copy(2 * stage + side, turned.at[turned_rows(turned, side, 1 - here.core)], taken.at[side])
-        for stage, turned, taken in ((1, act_t, act_mate), (0, input_t, input_mate))
-        for side in (0, 1)
+        mate_copy(0, input_mate, input_mate),
+        mate_copy(1, act_mate, act_mate),
+        mate_copy(2, x1.at[body], da1_mate),
+        mate_copy(3, x2.at[body], da2_mate),
     ]
-    mates.append(mate_copy(4, x2.at[pl.ds(1, rows)], da2_mate))
-    mates.append(mate_copy(5, x1.at[pl.ds(1, rows)], da1_mate))
-    for copy in mates[:4]:
-        copy.start()
-
-    for j in range(1, n_lead):
-        source = (here.lead + j) % n_lead
-        for piece in range(len(pieces)):
-            lead_copy(source, source, piece).wait_recv()
+
+    lead_group.wait_recv()
     parts_in[here.lead] = part[here.lead]
     for row in range(rows):
         total = parts_in[0, row].astype(F32)
@@ -454,19 +474,23 @@
     halo_2.start_rows()
     halo_2.take_edges()
     halo_2.start_columns()
-    mates[4].start()
-
-    def share_copy(stage, sent, taken, send_seat, recv_seat):
+    mates[3].start()
+
+    def share_copy(stage, sent, taken, send_seat, recv_seat, device=None):
         return pltpu.make_async_remote_copy(
             src_ref=sent.at[send_seat],
             dst_ref=taken.at[recv_seat],
-            send_sem=p1_send.at[stage, send_seat],
-            recv_sem=p1_recv.at[stage, recv_seat],
-            device_id=here.seat_device(send_seat),
+            send_sem=p1_send.at[stage],
+            recv_sem=p1_recv.at[stage],
+            device_id=here.seat_device(send_seat) if device is None else device,
             device_id_type=MESH,
         )
 
-    def weight_grad(stage, turned, turned_mate, da, da_mate, sent, taken, waits):
+    def share_group(stage, sent, taken):
+        every = pl.ds(0, seats - 1)
+        return share_copy(stage, sent, taken, every, every, here.near(0, 1))
+
+    def weight_grad(stage, turned, turned_mate, da, da_mate, sent, taken):
         share = sent.shape[1] * 2 // half
 
         @pl.loop(0, 2)
@@ -476,8 +500,8 @@
 
             @pl.when(j == 0)
             def _():
-                for number in waits:
-                    mates[number].wait_recv()
+                mates[stage].wait_recv()
+                mates[2 + stage].wait_recv()
 
             product += matmul(turned_mate[side], da_mate[...].reshape(da.shape), NN)
             for lon in range(n_lon):
@@ -500,11 +524,7 @@
     def plane_sum(stage, sent, taken):
         taken[here.seat] = sent[here.seat]
 
-        @pl.loop(1, seats)
-        def _(j):
-            seat = (here.seat + j) % seats
-            share_copy(stage, sent, taken, seat, seat).wait_recv()
-
+        share_group(stage, sent, taken).wait_recv()
         total = taken[0].astype(F32)
         for seat in range(1, seats):
             total += taken[seat].astype(F32)
@@ -514,8 +534,8 @@
         return pltpu.make_async_remote_copy(
             src_ref=sent.at[t],
             dst_ref=taken.at[slot],
-            send_sem=p2_send.at[stage, t],
-            recv_sem=p2_recv.at[stage, slot],
+            send_sem=p2_send.at[stage],
+            recv_sem=p2_recv.at[stage],
             device_id=here.plane_device(z),
             device_id_type=MESH,
         )
@@ -533,12 +553,27 @@
         def _():
             taken[here.z // 2] = sent[here.z % half // 2]
 
+    def plane_group(stage, sent, taken, own, act):
+        count = half // 2 if act == "wait_send" else half
+        for less in (0, 1):
+            every = pl.ds(0, count - less)
+            ref = sent.at[every] if act == "wait_send" else taken.at[every]
+            group = pltpu.make_async_remote_copy(
+                src_ref=ref,
+                dst_ref=ref,
+                send_sem=p2_send.at[stage],
+                recv_sem=p2_recv.at[stage],
+                device_id=here.near(0, 1),
+                device_id_type=MESH,
+            )
+            pl.when(own if less else jnp.logical_not(own))(getattr(group, act))
+
     def last_copy(stage, sent, taken, lead, slot):
         return pltpu.make_async_remote_copy(
             src_ref=sent,
             dst_ref=taken.at[slot],
-            send_sem=p3_send.at[stage, lead],
-            recv_sem=p3_recv.at[stage, slot],
+            send_sem=p3_send.at[stage],
+            recv_sem=p3_recv.at[stage],
             device_id=here.lead_device(lead),
             device_id_type=MESH,
         )
@@ -546,10 +581,7 @@
     def send_last(stage, sent, taken, last, last_taken):
         @pl.when(gathers)
         def _():
-            for j in range(half):
-                z = 2 * j + first_source
-                copy = plane_copy(stage, sent, taken, 0, j, z)
-                pl.when(z != here.z)(copy.wait_recv)
+            plane_group(stage, sent, taken, here.far == 0, "wait_recv")
             total = taken[0].astype(F32)
             for j in range(1, half):
                 total += taken[j].astype(F32)
@@ -558,17 +590,30 @@
                 last_copy(stage, last, last_taken, (here.lead + j) % n_lead, here.far).start()
             last_taken[here.far] = total
 
-    def final_sum(stage, last, last_taken, out):
-        for far in (0, 1):
-            source = 2 * far + here.z // half
-            copy = last_copy(stage, last, last_taken, source, far)
-            pl.when(source != here.lead)(copy.wait_recv)
-        out[...] = (last_taken[0] + last_taken[1]) * norm
+    def last_group(stage, last_taken, count):
+        every = last_taken.at[pl.ds(0, count)]
+        return pltpu.make_async_remote_copy(
+            src_ref=every,
+            dst_ref=every,
+            send_sem=p3_send.at[stage],
+            recv_sem=p3_recv.at[stage],
+            device_id=here.near(0, 1),
+            device_id_type=MESH,
+        )
+
+    def out_copy(stage, last_taken, out):
+        return pltpu.make_async_copy(last_taken.at[2], out, load_sem.at[8 + stage])
+
+    def final_sum(stage, last_taken, out):
+        pl.when(gathers)(last_group(stage, last_taken, 1).wait_recv)
+        pl.when(jnp.logical_not(gathers))(last_group(stage, last_taken, 2).wait_recv)
+        last_taken[2] = (last_taken[0] + last_taken[1]) * norm
+        out_copy(stage, last_taken, out).start()
 
     def tile(field):
         return field[pl.ds(1, rows)].reshape(cells, field.shape[-1])
 
-    weight_grad(1, act_t, act_mate, tile(x2), da2_mate, s1b, q1b, (0, 1, 4))
+    weight_grad(1, act_t, act_mate, tile(x2), da2_mate, s1b, q1b)
 
     ready("w_two")
     halo_2.wait_recv()
@@ -581,8 +626,8 @@
     halo_1.start_rows()
     halo_1.take_edges()
     halo_1.start_columns()
-    mates[5].start()
-    weight_grad(0, input_t, input_mate, tile(x1), da1_mate, s1a, q1a, (2, 3, 5))
+    mates[2].start()
+    weight_grad(0, input_t, input_mate, tile(x1), da1_mate, s1a, q1a)
 
     send_planes(1, plane_sum(1, s1b, q1b), s2b, q2b)
 
@@ -593,47 +638,31 @@
     for k, (u, v) in enumerate(OFFSETS):
         total += matmul(window(x1, x12, -u, -v, rows), w_one[k], NT)
     grad_stage[...] = total.astype(BF).reshape(grad_stage.shape)
-    stores = [
-        pltpu.make_async_copy(grad_stage.at[row], grad_out.at[:, row], load_sem.at[row])
-        for row in range(rows)
-    ]
-    for copy in stores:
-        copy.start()
+    for row in range(rows):
+        load("out", grad_stage.at[row], grad_out.at[:, row])
 
     send_planes(0, plane_sum(0, s1a, q1a), s2a, q2a)
     send_last(1, s2b, q2b, s3b, q3b)
     send_last(0, s2a, q2a, s3a, q3a)
-    for copy in stores:
-        copy.wait()
+    ready("out")
     for halo in (halo_h, halo_p, halo_e, halo_2, halo_1):
         halo.wait_send()
-
     for copy in mates:
         copy.wait_send()
-    for j in range(1, n_lead):
-        for piece in range(len(pieces)):
-            lead_copy(here.lead, (here.lead + j) % n_lead, piece).wait_send()
-
-    for stage, sent, taken in ((1, s1b, q1b), (0, s1a, q1a)):
-
-        @pl.loop(1, seats)
-        def _(j):
-            seat = (here.seat + j) % seats
-            share_copy(stage, sent, taken, seat, here.seat).wait_send()
-
-    final_sum(1, s3b, q3b, second_out)
-    final_sum(0, s3a, q3a, first_out)
-    for stage, sent, taken in ((1, s2b, q2b), (0, s2a, q2a)):
-        for t in range(half // 2):
-            z = first_target + 2 * t
-            copy = plane_copy(stage, sent, taken, t, here.z // 2, z)
-            pl.when(z != here.z)(copy.wait_send)
-
+    lead_group.wait_send()
+    share_group(1, s1b, q1b).wait_send()
+    share_group(0, s1a, q1a).wait_send()
+    plane_group(1, s2b, q2b, own_share, "wait_send")
+    plane_group(0, s2a, q2a, own_share, "wait_send")
+    final_sum(1, q3b, second_out)
+    final_sum(0, q3a, first_out)
     @pl.when(gathers)
     def _():
-        for stage, last, last_taken in ((1, s3b, q3b), (0, s3a, q3a)):
-            for j in range(1, n_lead):
-                last_copy(stage, last, last_taken, (here.lead + j) % n_lead, here.far).wait_send()
+        last_group(1, q3b, n_lead - 1).wait_send()
+        last_group(0, q3a, n_lead - 1).wait_send()
+
+    out_copy(1, q3b, second_out).wait()
+    out_copy(0, q3a, first_out).wait()
 
 
 def per_device(head_grads, head_weights, encoder_input, pre_first, pre_second, w_first, w_second):
@@ -667,7 +696,7 @@
             pltpu.VMEM((half // 2, share, width), BF),
             pltpu.VMEM((half, share, width), BF),
             pltpu.VMEM((share, width), F32),
-            pltpu.VMEM((2, share, width), F32),
+            pltpu.VMEM((3, share, width), F32),
         )
 
     own = (rows, samples, cols, width)
@@ -695,22 +724,16 @@
         *reduce_buffers(last_two),
         *reduce_buffers(last_one),
         pltpu.VMEM((rows, samples, cols, in_width), BF),
-        pltpu.SemaphoreType.DMA((64,)),
-        pltpu.SemaphoreType.DMA((5, 16)),
-        pltpu.SemaphoreType.DMA((5, 16)),
-        pltpu.SemaphoreType.DMA((n_lead, 3)),
-        pltpu.SemaphoreType.DMA((n_lead, 3)),
-        pltpu.SemaphoreType.DMA((6,)),
-        pltpu.SemaphoreType.DMA((6,)),
-        pltpu.SemaphoreType.DMA((2, seats)),
-        pltpu.SemaphoreType.DMA((2, seats)),
-        pltpu.SemaphoreType.DMA((2, half // 2)),
-        pltpu.SemaphoreType.DMA((2, half)),
-        pltpu.SemaphoreType.DMA((2, n_lead)),
-        pltpu.SemaphoreType.DMA((2, 2)),
+        pltpu.SemaphoreType.DMA((10,)),
+        pltpu.SemaphoreType.DMA((5, 5)),
+        pltpu.SemaphoreType.DMA((5, 5)),
+        pltpu.SemaphoreType.DMA((1,)),
+        pltpu.SemaphoreType.DMA((1,)),
+        pltpu.SemaphoreType.DMA((4,)),
+        pltpu.SemaphoreType.DMA((4,)),
+        *[pltpu.SemaphoreType.DMA((2,)) for _ in range(6)],
     ]
     anywhere = pl.BlockSpec(memory_space=pl.ANY)
-    vmem = pl.BlockSpec(memory_space=pltpu.VMEM)
     input_grad, grad_first, grad_second = pl.pallas_call(
         functools.partial(kernel, 1.0 / math.sqrt(cells_total)),
         out_shape=(
@@ -719,7 +742,7 @@
             jax.ShapeDtypeStruct((last_two, width), F32),
         ),
         in_specs=[anywhere] * 7,
-        out_specs=(anywhere, vmem, vmem),
+        out_specs=[anywhere] * 3,
         scratch_shapes=scratch,
         compiler_params=pltpu.CompilerParams(
             collective_id=0, has_side_effects=True, vmem_limit_bytes=56 * 2**20

time: 62.4 us -> 59.6 us (0.955)
  Pallas kernels: 57 us -> 54.5 us
    pallas_call x1, Pallas kernels: 57 us -> 54.5 us  [per_device(): pl.pallas_call(functools.partial(kernel, 1.0 / math.sqrt(cells_total)), o...]
where the time goes in v4:
time: 59.6 us; the launch traced here: 59.3 us
  Pallas kernels  54.5 us (91%)
  local copies, waits for them, and re-layouts  4.14 us (7%)
  between operations  0.64 us (1%)
    pallas_call x1, Pallas kernels, per_device(): pl.pallas_call(functools.partial(kernel, 1.0 / math.sqrt(cells_total)), o...  54.5 us
    reshape x2, local copies, waits for them, and re-layouts, per_device(): return (input_grad, grad_first.reshape(-1), grad_second.reshape(-1))  2.66 us
    unnamed x1, local copies, waits for them, and re-layouts  1.47 us

profile of v4, /device:TPU:1, one launch (start us, length us, event | category | flops | bytes accessed | tf_op | source)
XLA Modules:
  0.0 59.3 jit_solution(1594402691941711372)
XLA Ops:
  0.6 54.5 %shard_map.94 = (bf16[2,4,32,128]{3,2,1,0:T(8,128)(2,1)}, f32[9,256]{1,0:T(8,128)}, f32[18,256]{1,0:T(8,128)}) custom-call(bf16[2,8,4,32,128]{4,3,2,1,0:T(8,128)(2,1)} %heads_hbm.1, bf16[2,9,256,128]{3,2,1,0:T(8,128)(2,1)} %head_w_hbm.1, bf16[2,4,32,128]{3,2,1,0:T(8,128)(2,1)} %input_hbm.1, bf16[2,4,32,256]{3,2,1,0:T(8,128)(2,1)} %first_hbm.1, ...), custom_call_target="tpu_custom_call" | custom-call | tf_op jit(solution)/shard_map/pallas_call | solution.py:737
  55.2 1.3 %reshape.12 = f32[2304]{0:T(1024)} reshape(f32[9,256]{1,0:T(8,128)} %get-tuple-element.7) | data formatting | bytes 18432 | tf_op jit(solution)/shard_map/reshape | solution.py:751
  56.5 1.3 %reshape.13 = f32[4608]{0:T(1024)} reshape(f32[18,256]{1,0:T(8,128)} %get-tuple-element.8) | data formatting | bytes 36864 | tf_op jit(solution)/shard_map/reshape | solution.py:751
  57.9 1.5 %copy.11 = bf16[2,4,32,128]{3,2,1,0:T(8,128)(2,1)} copy(bf16[2,4,32,128]{3,2,1,0:T(8,128)(2,1)} %get-tuple-element.12) | data formatting | bytes 131072

commit v5 on v4

--- a/solution.py
+++ b/solution.py
@@ -601,14 +601,10 @@
             device_id_type=MESH,
         )
 
-    def out_copy(stage, last_taken, out):
-        return pltpu.make_async_copy(last_taken.at[2], out, load_sem.at[8 + stage])
-
     def final_sum(stage, last_taken, out):
         pl.when(gathers)(last_group(stage, last_taken, 1).wait_recv)
         pl.when(jnp.logical_not(gathers))(last_group(stage, last_taken, 2).wait_recv)
-        last_taken[2] = (last_taken[0] + last_taken[1]) * norm
-        out_copy(stage, last_taken, out).start()
+        out[...] = (last_taken[0] + last_taken[1]) * norm
 
     def tile(field):
         return field[pl.ds(1, rows)].reshape(cells, field.shape[-1])
@@ -660,9 +656,6 @@
     def _():
         last_group(1, q3b, n_lead - 1).wait_send()
         last_group(0, q3a, n_lead - 1).wait_send()
-
-    out_copy(1, q3b, second_out).wait()
-    out_copy(0, q3a, first_out).wait()
 
 
 def per_device(head_grads, head_weights, encoder_input, pre_first, pre_second, w_first, w_second):
@@ -724,7 +717,7 @@
         *reduce_buffers(last_two),
         *reduce_buffers(last_one),
         pltpu.VMEM((rows, samples, cols, in_width), BF),
-        pltpu.SemaphoreType.DMA((10,)),
+        pltpu.SemaphoreType.DMA((8,)),
         pltpu.SemaphoreType.DMA((5, 5)),
         pltpu.SemaphoreType.DMA((5, 5)),
         pltpu.SemaphoreType.DMA((1,)),
@@ -742,10 +735,10 @@
             jax.ShapeDtypeStruct((last_two, width), F32),
         ),
         in_specs=[anywhere] * 7,
-        out_specs=[anywhere] * 3,
+        out_specs=[anywhere] + [pl.BlockSpec(memory_space=pltpu.VMEM)] * 2,
         scratch_shapes=scratch,
         compiler_params=pltpu.CompilerParams(
-            collective_id=0, has_side_effects=True, vmem_limit_bytes=56 * 2**20
+            collective_id=0, has_side_effects=True, vmem_limit_bytes=55091 * 1024
         ),
     )(head_grads, head_weights, encoder_input, pre_first, pre_second, w_first, w_second)
     return input_grad, grad_first.reshape(-1), grad_second.reshape(-1)

time: 59.6 us -> 56.6 us (0.950)
  local copies, waits for them, and re-layouts: 4.14 us -> 1.84 us
  Pallas kernels: 54.5 us -> 53.9 us
    reshape x2, local copies, waits for them, and re-layouts: 2.66 us -> 1.21 us  [per_device(): return (input_grad, grad_first.reshape(-1), grad_second.reshape(-1))]
    unnamed x1, local copies, waits for them, and re-layouts: 1.47 us -> 0.63 us
    pallas_call x1, Pallas kernels: 54.5 us -> 53.9 us  [per_device(): pl.pallas_call(functools.partial(kernel, 1.0 / math.sqrt(cells_total)), o...]
where the time goes in v5:
time: 56.6 us; the launch traced here: 56.4 us
  Pallas kernels  53.9 us (95%)
  local copies, waits for them, and re-layouts  1.84 us (3%)
  between operations  0.64 us (1%)
    pallas_call x1, Pallas kernels, per_device(): pl.pallas_call(functools.partial(kernel, 1.0 / math.sqrt(cells_total)), o...  53.9 us
    reshape x2, local copies, waits for them, and re-layouts, per_device(): return (input_grad, grad_first.reshape(-1), grad_second.reshape(-1))  1.21 us

profile of v5, /device:TPU:1, one launch (start us, length us, event | category | flops | bytes accessed | tf_op | source)
XLA Modules:
  0.0 56.4 jit_solution(69036229273744123)
XLA Ops:
  0.6 53.9 %shard_map.94 = (bf16[2,4,32,128]{3,2,1,0:T(8,128)(2,1)S(1)}, f32[9,256]{1,0:T(8,128)S(1)}, f32[18,256]{1,0:T(8,128)S(1)}) custom-call(bf16[2,8,4,32,128]{4,3,2,1,0:T(8,128)(2,1)} %heads_hbm.1, bf16[2,9,256,128]{3,2,1,0:T(8,128)(2,1)} %head_w_hbm.1, bf16[2,4,32,128]{3,2,1,0:T(8,128)(2,1)} %input_hbm.1, bf16[2,4,32,256]{3,2,1,0:T(8,128)(2,1)} %first_hbm.1, ...), custom_call_target="tpu_custom_call" | custom-call | tf_op jit(solution)/shard_map/pallas_call | solution.py:730
  54.6 0.6 %reshape.12 = f32[2304]{0:T(1024)} reshape(f32[9,256]{1,0:T(8,128)S(1)} %get-tuple-element.7) | data formatting | bytes 18432 | tf_op jit(solution)/shard_map/reshape | solution.py:744
  55.2 0.6 %reshape.13 = f32[4608]{0:T(1024)} reshape(f32[18,256]{1,0:T(8,128)S(1)} %get-tuple-element.8) | data formatting | bytes 36864 | tf_op jit(solution)/shard_map/reshape | solution.py:744
  55.8 0.6 %copy.11 = bf16[2,4,32,128]{3,2,1,0:T(8,128)(2,1)} copy(bf16[2,4,32,128]{3,2,1,0:T(8,128)(2,1)S(1)} %get-tuple-element.12) | data formatting | bytes 131072

commit v6 on v5

--- a/solution.py
+++ b/solution.py
@@ -236,10 +236,10 @@
     pre_two, slope_two, slope_one, w_one, w_two,
     part, parts_in,
     act_t, input_t, act_mate, input_mate, da2_mate, da1_mate,
-    s1b, q1b, s2b, q2b, s3b, q3b, s1a, q1a, s2a, q2a, s3a, q3a,
+    along_y, from_y, along_x, from_x, then_x, last_x, then_y, last_y, s2b, q2b, s3b, q3b, s1a, q1a, s2a, q2a, s3a, q3a,
     grad_stage,
     load_sem, halo_send, halo_recv, lead_send, lead_recv, mate_send, mate_recv,
-    p1_send, p1_recv, p2_send, p2_recv, p3_send, p3_recv,
+    line_send, line_recv, p1_send, p1_recv, p2_send, p2_recv, p3_send, p3_recv, token,
 ):
     here = Place()
     n_lead, planes, n_lon, seats = here.n_lead, here.planes, here.n_lon, here.seats
@@ -261,36 +261,48 @@
 
         pl.when(has)(greet_rows)
 
-    for col in (-1, 1):
+    for col in (-1, 1, 2):
         greet(here.near(0, col))
+    x_here = 2 * here.far + here.side
+
+    def x_device(x):
+        return (2 * (x // 2) + here.core, x % 2 * planes + here.z, here.lon)
+
+    def z_device(step):
+        return here.plane_device((here.z + step + planes) % planes)
+
+    for step in (1, 3):
+        greet(x_device((x_here + step) % 4))
+    for step in (-1, 1):
+        greet(z_device(step))
     for j in range(1, n_lead):
         greet(here.lead_device((here.lead + j) % n_lead))
 
-    @pl.loop(1, seats)
-    def _(j):
-        greet(here.seat_device((here.seat + j) % seats))
+    greetings = (
+        3 + 2 + 2 + (n_lead - 1)
+        + jnp.where(here.has_low, 3, 0)
+        + jnp.where(here.has_high, 3, 0)
+    )
+
+    def send_token(number, device):
+        pl.semaphore_signal(token.at[number], inc=1, device_id=device, device_id_type=MESH)
+
+    def send_plane_tokens():
+        for number, step in enumerate((-1, 1, 2)):
+            send_token(number, here.near(0, step))
+
+    def send_z_tokens(level):
+        for number, step in enumerate((-1, 1)):
+            send_token(3 + 2 * level + number, z_device(step * 2**level))
+
+    def wait_tokens(*numbers):
+        for number in numbers:
+            pl.semaphore_wait(token.at[number], 1)
 
     gathers = here.z // half == here.core
     first_source = (here.z + here.far) % 2
     first_target = here.core * half + first_source
-
-    @pl.when(gathers)
-    def _():
-        @pl.loop(0, half)
-        def _(j):
-            z = 2 * j + first_source
-
-            @pl.when(z != here.z)
-            def _():
-                greet(here.plane_device(z))
-
     own_share = jnp.logical_and(gathers, here.far == 0)
-    greetings = (
-        2 + (n_lead - 1) + (seats - 1) + half // 2
-        + jnp.where(here.has_low, 3, 0)
-        + jnp.where(here.has_high, 3, 0)
-        - jnp.where(own_share, 1, 0)
-    )
 
     names = ("heads", "first", "input", "head_w", "second", "w_two", "w_one", "out")
     body = pl.ds(1, rows)
@@ -354,6 +366,8 @@
     halo_1.clear()
     pl.semaphore_wait(barrier, greetings)
     halo_h.start_rows()
+    send_plane_tokens()
+    send_z_tokens(0)
     ready("heads")
     halo_h.take_edges()
     halo_h.start_columns()
@@ -417,6 +431,9 @@
             part[owner, (rows - 1) * high] = block[owner * samples : (owner + 1) * samples]
         for j in (2, 3, 1):
             lead_copy(here.lead, (here.lead + j) % n_lead, 1 + high).start()
+
+    wait_tokens(3, 4)
+    send_z_tokens(1)
 
     ready("second")
     for row in range(rows):
@@ -475,6 +492,107 @@
     halo_2.take_edges()
     halo_2.start_columns()
     mates[3].start()
+    wait_tokens(5, 6)
+    send_z_tokens(2)
+    wait_tokens(0, 1, 2)
+
+    def weight_grad(stage, turned, turned_mate, da, da_mate, share, put, send):
+        @pl.loop(0, 2)
+        def _(j):
+            side = (here.side + 1 + j) % 2
+            product = matmul(turned[turned_rows(turned, side, here.core)], da, NN)
+
+            @pl.when(j == 0)
+            def _():
+                mates[stage].wait_recv()
+                mates[2 + stage].wait_recv()
+
+            product += matmul(turned_mate[side], da_mate[...].reshape(da.shape), NN)
+            for lon in range(n_lon):
+                for odd in (0, 1):
+                    far = (odd + here.z) % 2
+                    for t in range(half // 2):
+                        begin = ((2 * t + odd) * n_lon + lon) * share
+                        put(side, lon, far, t, product[begin : begin + share].astype(BF))
+            send(side)
+
+    quarter = half // 4
+
+    def lon_device(lon):
+        return (here.lead, here.lat, lon)
+
+    def line_copy(number, source, target, device):
+        return pltpu.make_async_remote_copy(
+            src_ref=source,
+            dst_ref=target,
+            send_sem=line_send.at[number],
+            recv_sem=line_recv.at[number],
+            device_id=device,
+            device_id_type=MESH,
+        )
+
+    lines = (
+        (along_y, from_y, here.lon, n_lon, lon_device),
+        (along_x, from_x, x_here, 4, x_device),
+        (then_x, last_x, x_here, 4, x_device),
+        (then_y, last_y, here.lon, n_lon, lon_device),
+    )
+
+    def line_send_to(number, there):
+        sent, taken, own, _, device = lines[number]
+        line_copy(number, sent.at[there], taken.at[own], device(there)).start()
+
+    def line_send_all(number):
+        _, _, own, count, _ = lines[number]
+        for j in range(1, count):
+            line_send_to(number, (own + j) % count)
+
+    def line_group(number):
+        sent, taken, _, count, _ = lines[number]
+        others = pl.ds(0, count - 1)
+        return line_copy(number, sent.at[others], taken.at[others], here.near(0, 1))
+
+    def line_take(number):
+        sent, taken, own, _, _ = lines[number]
+        line_group(number).wait_recv()
+        taken[own] = sent[own]
+
+    def put_second(side, lon, far, t, piece):
+        x = 2 * far + side
+        begin = t % quarter * piece.shape[0]
+        rows_there = slice(begin, begin + piece.shape[0])
+        if t < quarter:
+            along_y[lon, x, rows_there] = piece
+        else:
+            along_x[x, lon, rows_there] = piece
+
+    def send_second(side):
+        for far in (0, 1):
+            x = 2 * far + side
+            pl.when(x != x_here)(functools.partial(line_send_to, 1, x))
+
+    def pass_second():
+        for number in (0, 1):
+            line_take(number)
+            _, taken, _, count, _ = lines[number]
+            sent = lines[2 + number][0]
+            for there in range(sent.shape[0]):
+                total = taken[0, there].astype(F32)
+                for source in range(1, count):
+                    total += taken[source, there].astype(F32)
+                sent[there] = total.astype(BF)
+            line_send_all(2 + number)
+
+    def second_sums(share):
+        pieces = []
+        for number in (2, 3):
+            line_take(number)
+            _, taken, _, count, _ = lines[number]
+            total = taken[0].astype(F32)
+            for source in range(1, count):
+                total += taken[source].astype(F32)
+            pieces += [total[t * share : (t + 1) * share] for t in range(quarter)]
+        return pieces
 
     def share_copy(stage, sent, taken, send_seat, recv_seat, device=None):
         return pltpu.make_async_remote_copy(
@@ -490,45 +608,27 @@
         every = pl.ds(0, seats - 1)
         return share_copy(stage, sent, taken, every, every, here.near(0, 1))
 
-    def weight_grad(stage, turned, turned_mate, da, da_mate, sent, taken):
-        share = sent.shape[1] * 2 // half
-
-        @pl.loop(0, 2)
-        def _(j):
-            side = (here.side + 1 + j) % 2
-            product = matmul(turned[turned_rows(turned, side, here.core)], da, NN)
-
-            @pl.when(j == 0)
+    def put_first(side, lon, far, t, piece):
+        begin = t * piece.shape[0]
+        s1a[here.seat_of(side, lon, far), begin : begin + piece.shape[0]] = piece
+
+    def send_first(side):
+        @pl.loop(0, 2 * n_lon)
+        def _(i):
+            seat = 2 * n_lon * side + (here.seat + 2 + i) % (2 * n_lon)
+
+            @pl.when(seat != here.seat)
             def _():
-                mates[stage].wait_recv()
-                mates[2 + stage].wait_recv()
-
-            product += matmul(turned_mate[side], da_mate[...].reshape(da.shape), NN)
-            for lon in range(n_lon):
-                for odd in (0, 1):
-                    far = (odd + here.z) % 2
-                    seat = here.seat_of(side, lon, far)
-                    for t in range(half // 2):
-                        begin = ((2 * t + odd) * n_lon + lon) * share
-                        piece = product[begin : begin + share].astype(BF)
-                        sent[seat, t * share : (t + 1) * share] = piece
-
-            @pl.loop(0, 2 * n_lon)
-            def _(i):
-                seat = 2 * n_lon * side + (here.seat + 2 + i) % (2 * n_lon)
-
-                @pl.when(seat != here.seat)
-                def _():
-                    share_copy(stage, sent, taken, seat, here.seat).start()
-
-    def plane_sum(stage, sent, taken):
+                share_copy(0, s1a, q1a, seat, here.seat).start()
+
+    def plane_sum(stage, sent, taken, share):
         taken[here.seat] = sent[here.seat]
 
         share_group(stage, sent, taken).wait_recv()
         total = taken[0].astype(F32)
         for seat in range(1, seats):
             total += taken[seat].astype(F32)
-        return total
+        return [total[t * share : (t + 1) * share] for t in range(half // 2)]
 
     def plane_copy(stage, sent, taken, t, slot, z):
         return pltpu.make_async_remote_copy(
@@ -540,10 +640,9 @@
             device_id_type=MESH,
         )
 
-    def send_planes(stage, total, sent, taken):
-        share = sent.shape[1]
+    def send_planes(stage, pieces, sent, taken):
         for t in range(half // 2):
-            sent[t] = total[t * share : (t + 1) * share].astype(BF)
+            sent[t] = pieces[t].astype(BF)
         for t in range(half // 2):
             z = first_target + 2 * t
             copy = plane_copy(stage, sent, taken, t, here.z // 2, z)
@@ -609,7 +708,8 @@
     def tile(field):
         return field[pl.ds(1, rows)].reshape(cells, field.shape[-1])
 
-    weight_grad(1, act_t, act_mate, tile(x2), da2_mate, s1b, q1b)
+    weight_grad(1, act_t, act_mate, tile(x2), da2_mate, s3b.shape[0], put_second, send_second)
+    line_send_all(0)
 
     ready("w_two")
     halo_2.wait_recv()
@@ -623,9 +723,8 @@
     halo_1.take_edges()
     halo_1.start_columns()
     mates[2].start()
-    weight_grad(0, input_t, input_mate, tile(x1), da1_mate, s1a, q1a)
-
-    send_planes(1, plane_sum(1, s1b, q1b), s2b, q2b)
+    weight_grad(0, input_t, input_mate, tile(x1), da1_mate, s3a.shape[0], put_first, send_first)
+    pass_second()
 
     ready("w_one")
     halo_1.wait_recv()
@@ -637,7 +736,9 @@
     for row in range(rows):
         load("out", grad_stage.at[row], grad_out.at[:, row])
 
-    send_planes(0, plane_sum(0, s1a, q1a), s2a, q2a)
+    wait_tokens(7, 8)
+    send_planes(1, second_sums(s3b.shape[0]), s2b, q2b)
+    send_planes(0, plane_sum(0, s1a, q1a, s3a.shape[0]), s2a, q2a)
     send_last(1, s2b, q2b, s3b, q3b)
     send_last(0, s2a, q2a, s3a, q3a)
     ready("out")
@@ -646,7 +747,8 @@
     for copy in mates:
         copy.wait_send()
     lead_group.wait_send()
-    share_group(1, s1b, q1b).wait_send()
+    for number in range(4):
+        line_group(number).wait_send()
     share_group(0, s1a, q1a).wait_send()
     plane_group(1, s2b, q2b, own_share, "wait_send")
     plane_group(0, s2a, q2a, own_share, "wait_send")
@@ -684,13 +786,14 @@
 
     def reduce_buffers(share):
         return (
-            pltpu.VMEM((seats, share * half // 2, width), BF),
-            pltpu.VMEM((seats, share * half // 2, width), BF),
             pltpu.VMEM((half // 2, share, width), BF),
             pltpu.VMEM((half, share, width), BF),
             pltpu.VMEM((share, width), F32),
             pltpu.VMEM((3, share, width), F32),
         )
+
+    def line_buffers(first, then):
+        return [pltpu.VMEM((first, then, last_two * half // 4, width), BF)] * 2
 
     own = (rows, samples, cols, width)
     act_field = field(samples, width)
@@ -714,7 +817,12 @@
         pltpu.VMEM((2, rows_one // 4, cells), BF),
         pltpu.VMEM(own, BF),
         pltpu.VMEM(own, BF),
+        *line_buffers(n_lon, 4),
+        *line_buffers(4, n_lon),
+        *[pltpu.VMEM((4, last_two * half // 4, width), BF)] * 2,
+        *[pltpu.VMEM((n_lon, last_two * half // 4, width), BF)] * 2,
         *reduce_buffers(last_two),
+        *[pltpu.VMEM((seats, last_one * half // 2, width), BF)] * 2,
         *reduce_buffers(last_one),
         pltpu.VMEM((rows, samples, cols, in_width), BF),
         pltpu.SemaphoreType.DMA((8,)),
@@ -724,7 +832,10 @@
         pltpu.SemaphoreType.DMA((1,)),
         pltpu.SemaphoreType.DMA((4,)),
         pltpu.SemaphoreType.DMA((4,)),
+        pltpu.SemaphoreType.DMA((4,)),
+        pltpu.SemaphoreType.DMA((4,)),
         *[pltpu.SemaphoreType.DMA((2,)) for _ in range(6)],
+        pltpu.SemaphoreType.REGULAR((9,)),
     ]
     anywhere = pl.BlockSpec(memory_space=pl.ANY)
     input_grad, grad_first, grad_second = pl.pallas_call(

time: 56.6 us -> 55.9 us (0.988)
  Pallas kernels: 53.9 us -> 53.2 us
    pallas_call x1, Pallas kernels: 53.9 us -> 53.2 us  [per_device(): pl.pallas_call(functools.partial(kernel, 1.0 / math.sqrt(cells_total)), o...]
where the time goes in v6:
time: 55.9 us; the launch traced here: 55.7 us
  Pallas kernels  53.2 us (95%)
  local copies, waits for them, and re-layouts  1.84 us (3%)
  between operations  0.64 us (1%)
    pallas_call x1, Pallas kernels, per_device(): pl.pallas_call(functools.partial(kernel, 1.0 / math.sqrt(cells_total)), o...  53.2 us
    reshape x2, local copies, waits for them, and re-layouts, per_device(): return (input_grad, grad_first.reshape(-1), grad_second.reshape(-1))  1.21 us

profile of v6, /device:TPU:1, one launch (start us, length us, event | category | flops | bytes accessed | tf_op | source)
XLA Modules:
  0.0 55.7 jit_solution(7133103425587400450)
XLA Ops:
  0.6 53.2 %shard_map.94 = (bf16[2,4,32,128]{3,2,1,0:T(8,128)(2,1)S(1)}, f32[9,256]{1,0:T(8,128)S(1)}, f32[18,256]{1,0:T(8,128)S(1)}) custom-call(bf16[2,8,4,32,128]{4,3,2,1,0:T(8,128)(2,1)} %heads_hbm.1, bf16[2,9,256,128]{3,2,1,0:T(8,128)(2,1)} %head_w_hbm.1, bf16[2,4,32,128]{3,2,1,0:T(8,128)(2,1)} %input_hbm.1, bf16[2,4,32,256]{3,2,1,0:T(8,128)(2,1)} %first_hbm.1, ...), custom_call_target="tpu_custom_call" | custom-call | tf_op jit(solution)/shard_map/pallas_call | solution.py:841
  53.9 0.6 %reshape.12 = f32[2304]{0:T(1024)} reshape(f32[9,256]{1,0:T(8,128)S(1)} %get-tuple-element.7) | data formatting | bytes 18432 | tf_op jit(solution)/shard_map/reshape | solution.py:855
  54.5 0.6 %reshape.13 = f32[4608]{0:T(1024)} reshape(f32[18,256]{1,0:T(8,128)S(1)} %get-tuple-element.8) | data formatting | bytes 36864 | tf_op jit(solution)/shard_map/reshape | solution.py:855
  55.1 0.6 %copy.11 = bf16[2,4,32,128]{3,2,1,0:T(8,128)(2,1)} copy(bf16[2,4,32,128]{3,2,1,0:T(8,128)(2,1)S(1)} %get-tuple-element.12) | data formatting | bytes 131072

commit v7 on v6

--- a/solution.py
+++ b/solution.py
@@ -455,6 +455,7 @@
         input_t[pl.ds(k * block.shape[1], block.shape[1])] = block.T
 
     mate = here.lead + 1 - 2 * here.core
+    far_same, far_mate = (here.lead + 2) % n_lead, (mate + 2) % n_lead
 
     def mate_copy(number, source, target):
         return pltpu.make_async_remote_copy(
@@ -684,10 +685,10 @@
             total = taken[0].astype(F32)
             for j in range(1, half):
                 total += taken[j].astype(F32)
-            last[...] = total
-            for j in range(1, n_lead):
-                last_copy(stage, last, last_taken, (here.lead + j) % n_lead, here.far).start()
-            last_taken[here.far] = total
+            last[...] = total.astype(BF)
+            for lead in (far_same, far_mate, mate):
+                last_copy(stage, last, last_taken, lead, here.far).start()
+            last_taken[here.far] = total.astype(BF)
 
     def last_group(stage, last_taken, count):
         every = last_taken.at[pl.ds(0, count)]
@@ -703,7 +704,7 @@
     def final_sum(stage, last_taken, out):
         pl.when(gathers)(last_group(stage, last_taken, 1).wait_recv)
         pl.when(jnp.logical_not(gathers))(last_group(stage, last_taken, 2).wait_recv)
-        out[...] = (last_taken[0] + last_taken[1]) * norm
+        out[...] = (last_taken[0].astype(F32) + last_taken[1].astype(F32)) * norm
 
     def tile(field):
         return field[pl.ds(1, rows)].reshape(cells, field.shape[-1])
@@ -737,10 +738,10 @@
         load("out", grad_stage.at[row], grad_out.at[:, row])
 
     wait_tokens(7, 8)
+    send_planes(0, plane_sum(0, s1a, q1a, s3a.shape[0]), s2a, q2a)
     send_planes(1, second_sums(s3b.shape[0]), s2b, q2b)
-    send_planes(0, plane_sum(0, s1a, q1a, s3a.shape[0]), s2a, q2a)
+    send_last(0, s2a, q2a, s3a, q3a)
     send_last(1, s2b, q2b, s3b, q3b)
-    send_last(0, s2a, q2a, s3a, q3a)
     ready("out")
     for halo in (halo_h, halo_p, halo_e, halo_2, halo_1):
         halo.wait_send()
@@ -752,12 +753,25 @@
     share_group(0, s1a, q1a).wait_send()
     plane_group(1, s2b, q2b, own_share, "wait_send")
     plane_group(0, s2a, q2a, own_share, "wait_send")
+    final_sum(0, q3a, first_out)
     final_sum(1, q3b, second_out)
-    final_sum(0, q3a, first_out)
     @pl.when(gathers)
     def _():
         last_group(1, q3b, n_lead - 1).wait_send()
         last_group(0, q3a, n_lead - 1).wait_send()
+
+
+def write_out(input_grad, grad_first, grad_second, grad_out, first_out, second_out, first, second, sem):
+    copies = [pltpu.make_async_copy(input_grad, grad_out, sem.at[0])]
+    copies[0].start()
+    for number, (grad, line, out) in enumerate(((grad_first, first, first_out), (grad_second, second, second_out))):
+        width = grad.shape[1]
+        for row in range(grad.shape[0]):
+            line[pl.ds(row * width, width)] = grad[row]
+        copies.append(pltpu.make_async_copy(line, out, sem.at[1 + number]))
+        copies[-1].start()
+    for copy in copies:
+        copy.wait()
 
 
 def per_device(head_grads, head_weights, encoder_input, pre_first, pre_second, w_first, w_second):
@@ -788,8 +802,8 @@
         return (
             pltpu.VMEM((half // 2, share, width), BF),
             pltpu.VMEM((half, share, width), BF),
-            pltpu.VMEM((share, width), F32),
-            pltpu.VMEM((3, share, width), F32),
+            pltpu.VMEM((share, width), BF),
+            pltpu.VMEM((3, share, width), BF),
         )
 
     def line_buffers(first, then):
@@ -852,7 +866,19 @@
             collective_id=0, has_side_effects=True, vmem_limit_bytes=55091 * 1024
         ),
     )(head_grads, head_weights, encoder_input, pre_first, pre_second, w_first, w_second)
-    return input_grad, grad_first.reshape(-1), grad_second.reshape(-1)
+    flat = [jax.ShapeDtypeStruct((grad.size,), F32) for grad in (grad_first, grad_second)]
+    return pl.pallas_call(
+        write_out,
+        out_shape=(jax.ShapeDtypeStruct(input_grad.shape, BF), *flat),
+        in_specs=[anywhere] + [pl.BlockSpec(memory_space=pltpu.VMEM)] * 2,
+        out_specs=(anywhere, anywhere, anywhere),
+        scratch_shapes=[
+            pltpu.VMEM(flat[0].shape, F32),
+            pltpu.VMEM(flat[1].shape, F32),
+            pltpu.SemaphoreType.DMA((3,)),
+        ],
+        compiler_params=pltpu.CompilerParams(vmem_limit_bytes=2**20),
+    )(input_grad, grad_first, grad_second)
 
 
 def solution(mesh):

time: 55.9 us -> 54.3 us (0.971)
  local copies, waits for them, and re-layouts: 1.84 us -> 0 us
    reshape x2 -> x0, local copies, waits for them, and re-layouts: 1.21 us -> none  [per_device(): return (input_grad, grad_first.reshape(-1), grad_second.reshape(-1))]
    pallas_call x0 -> x1, Pallas kernels: none -> 0.66 us  [per_device(): pl.pallas_call(write_out, out_shape=(jax.ShapeDtypeStruct(input_grad.shap...]
    unnamed x1 -> x0, local copies, waits for them, and re-layouts: 0.63 us -> none
where the time goes in v7:
time: 54.3 us; the launch traced here: 54.2 us
  Pallas kernels  53.5 us (99%)
  between operations  0.64 us (1%)
    pallas_call x1, Pallas kernels, per_device(): pl.pallas_call(functools.partial(kernel, 1.0 / math.sqrt(cells_total)), o...  52.9 us

profile of v7, /device:TPU:1, one launch (start us, length us, event | category | flops | bytes accessed | tf_op | source)
XLA Modules:
  0.0 54.2 jit_solution(11240225418270551081)
XLA Ops:
  0.6 52.9 %shard_map.94 = (bf16[2,4,32,128]{3,2,1,0:T(8,128)(2,1)S(1)}, f32[9,256]{1,0:T(8,128)S(1)}, f32[18,256]{1,0:T(8,128)S(1)}) custom-call(bf16[2,8,4,32,128]{4,3,2,1,0:T(8,128)(2,1)} %heads_hbm.1, bf16[2,9,256,128]{3,2,1,0:T(8,128)(2,1)} %head_w_hbm.1, bf16[2,4,32,128]{3,2,1,0:T(8,128)(2,1)} %input_hbm.1, bf16[2,4,32,256]{3,2,1,0:T(8,128)(2,1)} %first_hbm.1, ...), custom_call_target="tpu_custom_call" | custom-call | tf_op jit(solution)/shard_map/pallas_call | solution.py:855
  53.5 0.7 %shard_map.95 = (bf16[2,4,32,128]{3,2,1,0:T(8,128)(2,1)}, f32[2304]{0:T(1024)}, f32[4608]{0:T(1024)}) custom-call(bf16[2,4,32,128]{3,2,1,0:T(8,128)(2,1)S(1)} %get-tuple-element.6.input_grad, f32[9,256]{1,0:T(8,128)S(1)} %get-tuple-element.7.grad_first, f32[18,256]{1,0:T(8,128)S(1)} %get-tuple-element.8.grad_second), custom_call_target="tpu_custom_call" | custom-call | tf_op jit(solution)/shard_map/pallas_call | solution.py:870

commit v8 on v7

--- a/solution.py
+++ b/solution.py
@@ -131,7 +131,10 @@
         self.start(self.copies[: self.row_count])
 
     def start_columns(self):
-        self.start(self.copies[self.row_count :])
+        self.start(self.copies[self.row_count : self.row_count + 2])
+
+    def start_corners(self):
+        self.start(self.copies[self.row_count + 2 :])
 
     def wait_columns(self):
         self.columns.wait_recv()
@@ -234,7 +237,7 @@
     x2, x22, e2, r2,
     x1, x12, e1, r1,
     pre_two, slope_two, slope_one, w_one, w_two,
-    part, parts_in,
+    part, parts_in, edge_sum,
     act_t, input_t, act_mate, input_mate, da2_mate, da1_mate,
     along_y, from_y, along_x, from_x, then_x, last_x, then_y, last_y, s2b, q2b, s3b, q3b, s1a, q1a, s2a, q2a, s3a, q3a,
     grad_stage,
@@ -256,12 +259,11 @@
     for has, step in ((here.has_low, -1), (here.has_high, 1)):
 
         def greet_rows(step=step):
-            for col in (-1, 0, 1):
-                greet(here.near(step, col))
+            greet(here.near(step, 0))
 
         pl.when(has)(greet_rows)
 
-    for col in (-1, 1, 2):
+    for col in (-1, 1):
         greet(here.near(0, col))
     x_here = 2 * here.far + here.side
 
@@ -275,19 +277,28 @@
         greet(x_device((x_here + step) % 4))
     for step in (-1, 1):
         greet(z_device(step))
-    for j in range(1, n_lead):
-        greet(here.lead_device((here.lead + j) % n_lead))
+    mate = here.lead + 1 - 2 * here.core
+    far_same, far_mate = (here.lead + 2) % n_lead, (mate + 2) % n_lead
+    greet(here.lead_device(mate))
 
     greetings = (
-        3 + 2 + 2 + (n_lead - 1)
-        + jnp.where(here.has_low, 3, 0)
-        + jnp.where(here.has_high, 3, 0)
+        2 + 2 + 2 + 1
+        + jnp.where(here.has_low, 1, 0)
+        + jnp.where(here.has_high, 1, 0)
     )
 
     def send_token(number, device):
         pl.semaphore_signal(token.at[number], inc=1, device_id=device, device_id_type=MESH)
 
+    def send_first_tokens():
+        for number, step in ((9, -1), (10, 1)):
+            send_token(number, here.near(0, step))
+        for number, step in ((11, 1), (12, 3)):
+            send_token(number, x_device((x_here + step) % 4))
+        send_z_tokens(0)
+
     def send_plane_tokens():
+        send_token(13, here.lead_device(mate))
         for number, step in enumerate((-1, 1, 2)):
             send_token(number, here.near(0, step))
 
@@ -366,19 +377,24 @@
     halo_1.clear()
     pl.semaphore_wait(barrier, greetings)
     halo_h.start_rows()
-    send_plane_tokens()
-    send_z_tokens(0)
+    send_first_tokens()
     ready("heads")
     halo_h.take_edges()
     halo_h.start_columns()
+    wait_tokens(9, 10, 11, 12, 3, 4)
+    halo_h.start_corners()
+    send_plane_tokens()
+    send_z_tokens(1)
     ready("first")
     halo_p.take_edges()
     halo_p.start_rows()
     halo_p.start_columns()
+    halo_p.start_corners()
     ready("input")
     halo_e.take_edges()
     halo_e.start_rows()
     halo_e.start_columns()
+    halo_e.start_corners()
     ready("head_w")
 
     pieces = (pl.ds(1, rows - 2), pl.ds(0, 1), pl.ds(rows - 1, 1))
@@ -403,37 +419,42 @@
             device_id_type=MESH,
         )
 
-    def convolve(first, count, batch):
+    def convolve(first, count, batch, steps=(-1, 0, 1)):
         total = None
         for k, (u, v) in enumerate(OFFSETS):
-            term = matmul(window(xh, xh2, -u, -v, count, batch, first), head_w[k], NT)
-            total = term if total is None else total + term
-        return total.astype(BF)
+            if u in steps:
+                term = matmul(window(xh, xh2, -u, -v, count, batch, first), head_w[k], NT)
+                total = term if total is None else total + term
+        return total
+
+    everyone = pl.ds(0, batch_all)
 
     halo_h.wait_columns()
     halo_h.spread(xh, xh2, range(1, rows + 1))
+    wait_tokens(13)
+
     @pl.loop(0, 2)
     def _(j):
         far = (here.far + 1 + j) % 2
         block = convolve(1, rows - 2, pl.ds(far * 2 * samples, 2 * samples))
-        block = block.reshape((rows - 2, 2 * samples) + part.shape[3:])
+        block = block.astype(BF).reshape((rows - 2, 2 * samples) + part.shape[3:])
         for core in (0, 1):
             owner = 2 * far + core
             part[owner, pieces[0]] = block[:, core * samples : (core + 1) * samples]
             copy = lead_copy(here.lead, owner, 0)
             pl.when(owner != here.lead)(copy.start)
 
+    edge_sum[0] = convolve(0, 1, everyone, (-1, 0))
+    edge_sum[1] = convolve(rows - 1, 1, everyone, (0, 1))
     for high in (0, 1):
         halo_h.wait_side(high)
         halo_h.spread(xh, xh2, [(rows + 1) * high])
-        block = convolve((rows - 1) * high, 1, pl.ds(0, batch_all)).reshape((batch_all,) + part.shape[3:])
+        block = edge_sum[high] + convolve((rows - 1) * high, 1, everyone, (-1 if high else 1,))
+        block = block.astype(BF).reshape((batch_all,) + part.shape[3:])
         for owner in range(n_lead):
             part[owner, (rows - 1) * high] = block[owner * samples : (owner + 1) * samples]
         for j in (2, 3, 1):
             lead_copy(here.lead, (here.lead + j) % n_lead, 1 + high).start()
-
-    wait_tokens(3, 4)
-    send_z_tokens(1)
 
     ready("second")
     for row in range(rows):
@@ -454,9 +475,6 @@
         block = window(xe, xe2, u, v, rows)
         input_t[pl.ds(k * block.shape[1], block.shape[1])] = block.T
 
-    mate = here.lead + 1 - 2 * here.core
-    far_same, far_mate = (here.lead + 2) % n_lead, (mate + 2) % n_lead
-
     def mate_copy(number, source, target):
         return pltpu.make_async_remote_copy(
             src_ref=source,
@@ -492,6 +510,7 @@
     halo_2.start_rows()
     halo_2.take_edges()
     halo_2.start_columns()
+    halo_2.start_corners()
     mates[3].start()
     wait_tokens(5, 6)
     send_z_tokens(2)
@@ -723,6 +742,7 @@
     halo_1.start_rows()
     halo_1.take_edges()
     halo_1.start_columns()
+    halo_1.start_corners()
     mates[2].start()
     weight_grad(0, input_t, input_mate, tile(x1), da1_mate, s3a.shape[0], put_first, send_first)
     pass_second()
@@ -825,6 +845,7 @@
         pltpu.VMEM(w_second.shape, BF),
         pltpu.VMEM((n_lead,) + own, BF),
         pltpu.VMEM((n_lead,) + own, BF),
+        pltpu.VMEM((2, batch_all * cols, width), F32),
         pltpu.VMEM((rows_two, cells), BF),
         pltpu.VMEM((rows_one, cells), BF),
         pltpu.VMEM((2, rows_two // 4, cells), BF),
@@ -849,7 +870,7 @@
         pltpu.SemaphoreType.DMA((4,)),
         pltpu.SemaphoreType.DMA((4,)),
         *[pltpu.SemaphoreType.DMA((2,)) for _ in range(6)],
-        pltpu.SemaphoreType.REGULAR((9,)),
+        pltpu.SemaphoreType.REGULAR((14,)),
     ]
     anywhere = pl.BlockSpec(memory_space=pl.ANY)
     input_grad, grad_first, grad_second = pl.pallas_call(

time: 54.3 us -> 52.4 us (0.965)
  Pallas kernels: 53.5 us -> 51.7 us
    pallas_call x1, Pallas kernels: 52.9 us -> 51 us  [per_device(): pl.pallas_call(functools.partial(kernel, 1.0 / math.sqrt(cells_total)), o...]
where the time goes in v8:
time: 52.4 us; the launch traced here: 52.3 us
  Pallas kernels  51.7 us (99%)
  between operations  0.64 us (1%)
    pallas_call x1, Pallas kernels, per_device(): pl.pallas_call(functools.partial(kernel, 1.0 / math.sqrt(cells_total)), o...  51 us

profile of v8, /device:TPU:1, one launch (start us, length us, event | category | flops | bytes accessed | tf_op | source)
XLA Modules:
  0.0 52.3 jit_solution(2552417191961665819)
XLA Ops:
  0.6 51.0 %shard_map.94 = (bf16[2,4,32,128]{3,2,1,0:T(8,128)(2,1)S(1)}, f32[9,256]{1,0:T(8,128)S(1)}, f32[18,256]{1,0:T(8,128)S(1)}) custom-call(bf16[2,8,4,32,128]{4,3,2,1,0:T(8,128)(2,1)} %heads_hbm.1, bf16[2,9,256,128]{3,2,1,0:T(8,128)(2,1)} %head_w_hbm.1, bf16[2,4,32,128]{3,2,1,0:T(8,128)(2,1)} %input_hbm.1, bf16[2,4,32,256]{3,2,1,0:T(8,128)(2,1)} %first_hbm.1, ...), custom_call_target="tpu_custom_call" | custom-call | tf_op jit(solution)/shard_map/pallas_call | solution.py:876
  51.7 0.7 %shard_map.95 = (bf16[2,4,32,128]{3,2,1,0:T(8,128)(2,1)}, f32[2304]{0:T(1024)}, f32[4608]{0:T(1024)}) custom-call(bf16[2,4,32,128]{3,2,1,0:T(8,128)(2,1)S(1)} %get-tuple-element.6.input_grad, f32[9,256]{1,0:T(8,128)S(1)} %get-tuple-element.7.grad_first, f32[18,256]{1,0:T(8,128)S(1)} %get-tuple-element.8.grad_second), custom_call_target="tpu_custom_call" | custom-call | tf_op jit(solution)/shard_map/pallas_call | solution.py:891

commit v9 on v8

--- a/solution.py
+++ b/solution.py
@@ -237,7 +237,7 @@
     x2, x22, e2, r2,
     x1, x12, e1, r1,
     pre_two, slope_two, slope_one, w_one, w_two,
-    part, parts_in, edge_sum,
+    part, parts_in, edge_sum, own_product,
     act_t, input_t, act_mate, input_mate, da2_mate, da1_mate,
     along_y, from_y, along_x, from_x, then_x, last_x, then_y, last_y, s2b, q2b, s3b, q3b, s1a, q1a, s2a, q2a, s3a, q3a,
     grad_stage,
@@ -517,16 +517,17 @@
     wait_tokens(0, 1, 2)
 
     def weight_grad(stage, turned, turned_mate, da, da_mate, share, put, send):
+        block = turned.shape[0] // 4
+        for j in (0, 1):
+            side = (here.side + 1 + j) % 2
+            own_product[j, pl.ds(0, block)] = matmul(turned[turned_rows(turned, side, here.core)], da, NN)
+        mates[stage].wait_recv()
+        mates[2 + stage].wait_recv()
+
         @pl.loop(0, 2)
         def _(j):
             side = (here.side + 1 + j) % 2
-            product = matmul(turned[turned_rows(turned, side, here.core)], da, NN)
-
-            @pl.when(j == 0)
-            def _():
-                mates[stage].wait_recv()
-                mates[2 + stage].wait_recv()
-
+            product = own_product[j, pl.ds(0, block)]
             product += matmul(turned_mate[side], da_mate[...].reshape(da.shape), NN)
             for lon in range(n_lon):
                 for odd in (0, 1):
@@ -731,14 +732,28 @@
     weight_grad(1, act_t, act_mate, tile(x2), da2_mate, s3b.shape[0], put_second, send_second)
     line_send_all(0)
 
+    def second_layer(first, count, steps=(-1, 0, 1)):
+        total = None
+        for k, (u, v) in enumerate(OFFSETS):
+            if u in steps:
+                term = matmul(window(x2, x22, -u, -v, count, None, first), w_two[k], NT)
+                total = term if total is None else total + term
+        return total
+
+    def store_first(first, count, total):
+        slope = slope_one[pl.ds(first, count)]
+        x1[pl.ds(1 + first, count)] = (total.reshape(slope.shape) * slope).astype(BF)
+
     ready("w_two")
-    halo_2.wait_recv()
-    halo_2.spread(x2, x22)
-    total = jnp.zeros((cells, w_two.shape[1]), F32)
-    for k, (u, v) in enumerate(OFFSETS):
-        total += matmul(window(x2, x22, -u, -v, rows), w_two[k], NT)
-    da_first = total.reshape(slope_one.shape) * slope_one[...]
-    x1[pl.ds(1, rows)] = da_first.astype(BF)
+    halo_2.wait_columns()
+    halo_2.spread(x2, x22, range(1, rows + 1))
+    store_first(1, rows - 2, second_layer(1, rows - 2))
+    early = (second_layer(0, 1, (-1, 0)), second_layer(rows - 1, 1, (0, 1)))
+    halo_2.wait_side(0)
+    halo_2.wait_side(1)
+    halo_2.spread(x2, x22, (0, rows + 1))
+    store_first(0, 1, early[0] + second_layer(0, 1, (1,)))
+    store_first(rows - 1, 1, early[1] + second_layer(rows - 1, 1, (-1,)))
     halo_1.start_rows()
     halo_1.take_edges()
     halo_1.start_columns()
@@ -846,6 +861,7 @@
         pltpu.VMEM((n_lead,) + own, BF),
         pltpu.VMEM((n_lead,) + own, BF),
         pltpu.VMEM((2, batch_all * cols, width), F32),
+        pltpu.VMEM((2, rows_two // 4, width), F32),
         pltpu.VMEM((rows_two, cells), BF),
         pltpu.VMEM((rows_one, cells), BF),
         pltpu.VMEM((2, rows_two // 4, cells), BF),

time: 52.4 us -> 52.3 us (level)
  no operation moved by 1% of the time
where the time goes in v9:
time: 52.3 us; the launch traced here: 52.2 us
  Pallas kernels  51.5 us (98%)
  between operations  0.64 us (1%)
    pallas_call x1, Pallas kernels, per_device(): pl.pallas_call(functools.partial(kernel, 1.0 / math.sqrt(cells_total)), o...  50.9 us

profile of v9, /device:TPU:1, one launch (start us, length us, event | category | flops | bytes accessed | tf_op | source)
XLA Modules:
  0.0 52.2 jit_solution(8634302764655262278)
XLA Ops:
  0.6 50.9 %shard_map.94 = (bf16[2,4,32,128]{3,2,1,0:T(8,128)(2,1)S(1)}, f32[9,256]{1,0:T(8,128)S(1)}, f32[18,256]{1,0:T(8,128)S(1)}) custom-call(bf16[2,8,4,32,128]{4,3,2,1,0:T(8,128)(2,1)} %heads_hbm.1, bf16[2,9,256,128]{3,2,1,0:T(8,128)(2,1)} %head_w_hbm.1, bf16[2,4,32,128]{3,2,1,0:T(8,128)(2,1)} %input_hbm.1, bf16[2,4,32,256]{3,2,1,0:T(8,128)(2,1)} %first_hbm.1, ...), custom_call_target="tpu_custom_call" | custom-call | tf_op jit(solution)/shard_map/pallas_call | solution.py:892
  51.5 0.7 %shard_map.95 = (bf16[2,4,32,128]{3,2,1,0:T(8,128)(2,1)}, f32[2304]{0:T(1024)}, f32[4608]{0:T(1024)}) custom-call(bf16[2,4,32,128]{3,2,1,0:T(8,128)(2,1)S(1)} %get-tuple-element.6.input_grad, f32[9,256]{1,0:T(8,128)S(1)} %get-tuple-element.7.grad_first, f32[18,256]{1,0:T(8,128)S(1)} %get-tuple-element.8.grad_second), custom_call_target="tpu_custom_call" | custom-call | tf_op jit(solution)/shard_map/pallas_call | solution.py:907
